TPU v7x, 32 devices: a whole 2x2x4 slice. The times are simulated.
32 devices in a mesh: dp: 32 (over z, y, x, core).
Axes of the slice: x: 2, y: 2, z: 4, core: 2. Of those that a mesh axis runs over, the one named last changes fastest.
Arguments:
- features: bfloat16 [32768, 768], P('dp'), may hold values from -6 to 6
- pos_conv: bfloat16 [32768, 768], P('dp'), may hold values from -3 to 3
- segment_ids: int32 [32, 1024], P('dp'), may hold values from 0 to 3, never falling along the last dimension, each value on 1 to 512 neighbouring positions
- frame_valid: int32 [32, 1024], P('dp'), may hold values 0 or 1
- cotangent: bfloat16 [32768, 768], P('dp'), may hold values from -6 to 6
- qkv_weight: float32 [768, 2304], P('dp'), may hold values from -0.21875 to 0.21875
- proj_weight: float32 [768, 768], P('dp'), may hold values from -1.75 to 1.75
- expand_weight: float32 [768, 3072], P('dp'), may hold values from -0.21875 to 0.21875
- reduce_weight: float32 [3072, 768], P('dp'), may hold values from -0.109375 to 0.109375
- norm_gains: float32 [2, 768], P(None, 'dp'), may hold values from 0.5 to 1.5
- bias_vector: float32 [7680], P('dp'), may hold values from -1.5 to 1.5
- qkv_moment: float32 [768, 2304], P('dp'), may hold values from -1086.116 to 1086.116
- proj_moment: float32 [768, 768], P('dp'), may hold values from -108.6116 to 108.6116
- expand_moment: float32 [768, 3072], P('dp'), may hold values from -325.8348 to 325.8348
- reduce_moment: float32 [3072, 768], P('dp'), may hold values from -651.6696 to 651.6696
- gains_moment: float32 [2, 768], P(None, 'dp'), may hold values from -1086.116 to 1086.116
- bias_moment: float32 [7680], P('dp'), may hold values from -1086.116 to 1086.116
- qkv_average: float32 [768, 2304], P('dp'), may hold values from -0.21875 to 0.21875
- proj_average: float32 [768, 768], P('dp'), may hold values from -1.75 to 1.75
- expand_average: float32 [768, 3072], P('dp'), may hold values from -0.21875 to 0.21875
- reduce_average: float32 [3072, 768], P('dp'), may hold values from -0.109375 to 0.109375
- gains_average: float32 [2, 768], P(None, 'dp'), may hold values from 0.5 to 1.5
- bias_average: float32 [7680], P('dp'), may hold values from -1.5 to 1.5
Outputs:
- layer_out: bfloat16 [32768, 768], P('dp')
- grad_input: bfloat16 [32768, 768], P('dp')
- qkv_grad: float32 [768, 2304], P('dp')
- proj_grad: float32 [768, 768], P('dp')
- expand_grad: float32 [768, 3072], P('dp')
- reduce_grad: float32 [3072, 768], P('dp')
- gains_grad: float32 [2, 768], P(None, 'dp')
- bias_grad: float32 [7680], P('dp')
- qkv_master: float32 [768, 2304], P('dp')
- proj_master: float32 [768, 768], P('dp')
- expand_master: float32 [768, 3072], P('dp')
- reduce_master: float32 [3072, 768], P('dp')
- gains_master: float32 [2, 768], P(None, 'dp')
- bias_master: float32 [7680], P('dp')
- qkv_velocity: float32 [768, 2304], P('dp')
- proj_velocity: float32 [768, 768], P('dp')
- expand_velocity: float32 [768, 3072], P('dp')
- reduce_velocity: float32 [3072, 768], P('dp')
- gains_velocity: float32 [2, 768], P(None, 'dp')
- bias_velocity: float32 [7680], P('dp')
- qkv_smooth: float32 [768, 2304], P('dp')
- proj_smooth: float32 [768, 768], P('dp')
- expand_smooth: float32 [768, 3072], P('dp')
- reduce_smooth: float32 [3072, 768], P('dp')
- gains_smooth: float32 [2, 768], P(None, 'dp')
- bias_smooth: float32 [7680], P('dp')
Inputs may be any that keep to these rules, and one draw needn't show every extreme that they name: `segment_ids`: each row lists one device's utterances: numbers 0 to 3 in order, each a run of 1 to 512 frames, one of exactly 512. `frame_valid`: 1 marks a frame with audio.
All inputs are finite; a program needn't handle non-finite values. No bound on the sum of `frame_valid` on one device may be relied on, other than what follows from the above.
Results may differ from a plain program's by a relative error of at most 0.015.
The roundings to bfloat16 on the way count: a program that leaves them out, or rounds other values in their place, can miss the bound.
Values may be sent and summed in bfloat16 or wider, within the bound.
A program may use at most 320 MiB of HBM per device.

v0:
```python
import math

import jax
import jax.numpy as jnp
from jax import lax
from jax.sharding import PartitionSpec as P

D = 768
H = 12
HD = 64
FF = 3072


EPSILON = 1e-05
MASKED = -1000000000.0
rate_matrix = 0.04
rate_proj = 0.5
rate_small = 0.2


def layer_norm(residual, gain_row, offset):
    center = residual - jnp.mean(residual, axis=-1, keepdims=True)
    spread = jnp.mean(center * center, axis=-1, keepdims=True)
    return center * lax.rsqrt(spread + EPSILON) * gain_row + offset


def gelu_exact(argument):
    return 0.5 * argument * (1.0 + jax.scipy.special.erf(argument * 0.7071067811865476))


def masked_scores(queries, key_heads, segments, present, first_row, block_rows):
    query_part = queries[first_row : first_row + block_rows]
    scores = (
        jnp.einsum("qhe,khe->hqk", query_part, key_heads, preferred_element_type=jnp.float32)
        * 0.125
    )
    column = jnp.arange(key_heads.shape[0])
    row_ids = column[first_row : first_row + block_rows]
    allowed = (segments[first_row : first_row + block_rows, None] == segments[None, :]) & (
        (present[None, :] > 0) | (row_ids[:, None] == column[None, :])
    )
    return (jnp.where(allowed[None], scores, MASKED), query_part)


def nesterov(master, gradient, moment, average, step_rate):
    velocity = 0.5 * moment + gradient
    renewed = master - step_rate * (gradient + 0.5 * velocity)
    smooth = 0.5 * average + 0.5 * renewed
    return (renewed, velocity, smooth)


def local(
    features,
    pos_conv,
    segment_ids,
    frame_valid,
    cotangent,
    qkv_weight,
    proj_weight,
    expand_weight,
    reduce_weight,
    norm_gains,
    bias_vector,
    qkv_moment,
    proj_moment,
    expand_moment,
    reduce_moment,
    gains_moment,
    bias_moment,
    qkv_average,
    proj_average,
    expand_average,
    reduce_average,
    gains_average,
    bias_average,
):
    row_count = features.shape[0]
    block_rows = min(512, row_count)
    segments = segment_ids[0]
    present = frame_valid[0]
    valid_col = present.astype(jnp.float32)[:, None]
    qkv_full, proj_full, expand_full, reduce_full, gains_low, bias_low = (
        lax.all_gather(qkv_weight.astype(jnp.bfloat16), "dp", axis=0, tiled=True),
        lax.all_gather(proj_weight.astype(jnp.bfloat16), "dp", axis=0, tiled=True),
        lax.all_gather(expand_weight.astype(jnp.bfloat16), "dp", axis=0, tiled=True),
        lax.all_gather(reduce_weight.astype(jnp.bfloat16), "dp", axis=0, tiled=True),
        lax.all_gather(norm_gains.astype(jnp.bfloat16), "dp", axis=1, tiled=True),
        lax.all_gather(bias_vector.astype(jnp.bfloat16), "dp", axis=0, tiled=True),
    )
    gains_full = gains_low.astype(jnp.float32)
    bias_full = bias_low.astype(jnp.float32)
    bias_query = bias_full[0:D]
    bias_value = bias_full[D : 2 * D]
    bias_proj = bias_full[2 * D : 3 * D]
    bias_expand = bias_full[3 * D : 3 * D + FF]
    bias_reduce = bias_full[3 * D + FF : 4 * D + FF]
    offset_first = bias_full[4 * D + FF : 5 * D + FF]
    offset_second = bias_full[5 * D + FF : 6 * D + FF]
    entry_sum = (features.astype(jnp.float32) + pos_conv.astype(jnp.float32)) * valid_col
    entry_low = entry_sum.astype(jnp.bfloat16)
    qkv_bias = jnp.concatenate([bias_query, jnp.zeros((D,), jnp.float32), bias_value])
    qkv_rows = (jnp.dot(entry_low, qkv_full, preferred_element_type=jnp.float32) + qkv_bias).astype(
        jnp.bfloat16
    )
    shaped = qkv_rows.reshape(row_count, 3, H, HD)
    queries = shaped[:, 0]
    key_heads = shaped[:, 1]
    values = shaped[:, 2]
    pieces = []
    log_totals = []
    for first_row in range(0, row_count, block_rows):
        scores, query_part = masked_scores(
            queries, key_heads, segments, present, first_row, block_rows
        )
        maximum = jnp.max(scores, axis=-1, keepdims=True)
        exponent = jnp.exp(scores - maximum)
        row_total = jnp.sum(exponent, axis=-1, keepdims=True)
        weights_now = (exponent / row_total).astype(jnp.bfloat16)
        pieces.append(
            jnp.einsum("hqk,khe->qhe", weights_now, values, preferred_element_type=jnp.float32)
        )
        log_totals.append(maximum + jnp.log(row_total))
    context = jnp.concatenate(pieces, axis=0).reshape(row_count, D).astype(jnp.bfloat16)
    attended = jnp.dot(context, proj_full, preferred_element_type=jnp.float32) + bias_proj
    normed, first_norm_back = jax.vjp(layer_norm, entry_sum + attended, gains_full[0], offset_first)
    normed_low = normed.astype(jnp.bfloat16)
    pre_act = jnp.dot(normed_low, expand_full, preferred_element_type=jnp.float32) + bias_expand
    activated, gelu_back = jax.vjp(gelu_exact, pre_act)
    act_low = activated.astype(jnp.bfloat16)
    ffn_out = jnp.dot(act_low, reduce_full, preferred_element_type=jnp.float32) + bias_reduce
    layer_float, second_norm_back = jax.vjp(
        layer_norm, normed + ffn_out, gains_full[1], offset_second
    )
    layer_out = layer_float.astype(jnp.bfloat16)
    qkv_back, proj_back, expand_back, reduce_back = (
        lax.all_gather(qkv_weight.astype(jnp.bfloat16), "dp", axis=0, tiled=True),
        lax.all_gather(proj_weight.astype(jnp.bfloat16), "dp", axis=0, tiled=True),
        lax.all_gather(expand_weight.astype(jnp.bfloat16), "dp", axis=0, tiled=True),
        lax.all_gather(reduce_weight.astype(jnp.bfloat16), "dp", axis=0, tiled=True),
    )
    grad_second, grad_gain_two, grad_offset_two = second_norm_back(cotangent.astype(jnp.float32))
    grad_ffn = grad_second.astype(jnp.bfloat16)
    grad_bias_reduce = jnp.sum(grad_ffn, axis=0, dtype=jnp.float32)
    grad_reduce = jnp.einsum("tf,td->fd", act_low, grad_ffn, preferred_element_type=jnp.float32)
    grad_hidden = jnp.einsum("td,fd->tf", grad_ffn, reduce_back, preferred_element_type=jnp.float32)
    (grad_pre_float,) = gelu_back(grad_hidden)
    grad_pre = grad_pre_float.astype(jnp.bfloat16)
    grad_bias_expand = jnp.sum(grad_pre, axis=0, dtype=jnp.float32)
    grad_expand = jnp.einsum("td,tf->df", normed_low, grad_pre, preferred_element_type=jnp.float32)
    grad_normed = grad_second + jnp.einsum(
        "tf,df->td", grad_pre, expand_back, preferred_element_type=jnp.float32
    )
    grad_first, grad_gain_one, grad_offset_one = first_norm_back(grad_normed)
    grad_branch = grad_first.astype(jnp.bfloat16)
    grad_bias_proj = jnp.sum(grad_branch, axis=0, dtype=jnp.float32)
    grad_proj = jnp.einsum("td,te->de", context, grad_branch, preferred_element_type=jnp.float32)
    grad_context = jnp.einsum(
        "te,de->td", grad_branch, proj_back, preferred_element_type=jnp.float32
    )
    grad_context = grad_context.astype(jnp.bfloat16).reshape(row_count, H, HD)
    query_grads = []
    key_grad = jnp.zeros((row_count, H, HD), jnp.float32)
    value_grad = jnp.zeros((row_count, H, HD), jnp.float32)
    for block_index, first_row in enumerate(range(0, row_count, block_rows)):
        scores, query_part = masked_scores(
            queries, key_heads, segments, present, first_row, block_rows
        )
        prob_block = jnp.exp(scores - log_totals[block_index])
        context_part = grad_context[first_row : first_row + block_rows]
        prob_grad = jnp.einsum(
            "qhe,khe->hqk", context_part, values, preferred_element_type=jnp.float32
        )
        row_dot = jnp.sum(prob_block * prob_grad, axis=-1, keepdims=True)
        score_grad = (prob_block * (prob_grad - row_dot)).astype(jnp.bfloat16)
        query_grads.append(
            0.125
            * jnp.einsum("hqk,khe->qhe", score_grad, key_heads, preferred_element_type=jnp.float32)
        )
        key_grad = key_grad + 0.125 * jnp.einsum(
            "hqk,qhe->khe", score_grad, query_part, preferred_element_type=jnp.float32
        )
        value_grad = value_grad + jnp.einsum(
            "hqk,qhe->khe",
            prob_block.astype(jnp.bfloat16),
            context_part,
            preferred_element_type=jnp.float32,
        )
    grad_qkv_low = jnp.stack([jnp.concatenate(query_grads, axis=0), key_grad, value_grad], axis=1)
    grad_qkv_low = grad_qkv_low.reshape(row_count, 3 * D).astype(jnp.bfloat16)
    grad_bias_query = jnp.sum(grad_qkv_low[:, 0:D], axis=0, dtype=jnp.float32)
    grad_bias_value = jnp.sum(grad_qkv_low[:, 2 * D : 3 * D], axis=0, dtype=jnp.float32)
    grad_qkv = jnp.einsum("td,te->de", entry_low, grad_qkv_low, preferred_element_type=jnp.float32)
    grad_entry = grad_first + jnp.einsum(
        "te,de->td", grad_qkv_low, qkv_back, preferred_element_type=jnp.float32
    )
    grad_input = (grad_entry * valid_col).astype(jnp.bfloat16)
    grad_gains = jnp.stack([grad_gain_one, grad_gain_two], axis=0)
    grad_bias = jnp.concatenate(
        [
            grad_bias_query,
            grad_bias_value,
            grad_bias_proj,
            grad_bias_expand,
            grad_bias_reduce,
            grad_offset_one,
            grad_offset_two,
        ]
    )
    qkv_grad, proj_grad, expand_grad, reduce_grad, gains_grad, bias_grad = (
        lax.psum_scatter(grad_qkv, "dp", scatter_dimension=0, tiled=True),
        lax.psum_scatter(grad_proj, "dp", scatter_dimension=0, tiled=True),
        lax.psum_scatter(grad_expand, "dp", scatter_dimension=0, tiled=True),
        lax.psum_scatter(grad_reduce, "dp", scatter_dimension=0, tiled=True),
        lax.psum_scatter(grad_gains, "dp", scatter_dimension=1, tiled=True),
        lax.psum_scatter(grad_bias, "dp", scatter_dimension=0, tiled=True),
    )
    frame_total = lax.axis_size("dp") * row_count
    matrix_rate = rate_matrix / math.sqrt(frame_total)
    proj_step = rate_proj / math.sqrt(frame_total)
    small_step = rate_small / math.sqrt(frame_total)
    qkv_new = nesterov(qkv_weight, qkv_grad, qkv_moment, qkv_average, matrix_rate)
    proj_new = nesterov(proj_weight, proj_grad, proj_moment, proj_average, proj_step)
    expand_new = nesterov(expand_weight, expand_grad, expand_moment, expand_average, matrix_rate)
    reduce_new = nesterov(reduce_weight, reduce_grad, reduce_moment, reduce_average, matrix_rate)
    gains_new = nesterov(norm_gains, gains_grad, gains_moment, gains_average, small_step)
    bias_new = nesterov(bias_vector, bias_grad, bias_moment, bias_average, small_step)
    return (
        layer_out,
        grad_input,
        qkv_grad,
        proj_grad,
        expand_grad,
        reduce_grad,
        gains_grad,
        bias_grad,
        qkv_new[0],
        proj_new[0],
        expand_new[0],
        reduce_new[0],
        gains_new[0],
        bias_new[0],
        qkv_new[1],
        proj_new[1],
        expand_new[1],
        reduce_new[1],
        gains_new[1],
        bias_new[1],
        qkv_new[2],
        proj_new[2],
        expand_new[2],
        reduce_new[2],
        gains_new[2],
        bias_new[2],
    )


def solution(mesh):
    in_specs = (
        P("dp", None),
        P("dp", None),
        P("dp", None),
        P("dp", None),
        P("dp", None),
        P("dp", None),
        P("dp", None),
        P("dp", None),
        P("dp", None),
        P(None, "dp"),
        P("dp"),
        P("dp", None),
        P("dp", None),
        P("dp", None),
        P("dp", None),
        P(None, "dp"),
        P("dp"),
        P("dp", None),
        P("dp", None),
        P("dp", None),
        P("dp", None),
        P(None, "dp"),
        P("dp"),
    )
    out_specs = (
        P("dp", None),
        P("dp", None),
        P("dp", None),
        P("dp", None),
        P("dp", None),
        P("dp", None),
        P(None, "dp"),
        P("dp"),
        P("dp", None),
        P("dp", None),
        P("dp", None),
        P("dp", None),
        P(None, "dp"),
        P("dp"),
        P("dp", None),
        P("dp", None),
        P("dp", None),
        P("dp", None),
        P(None, "dp"),
        P("dp"),
        P("dp", None),
        P("dp", None),
        P("dp", None),
        P("dp", None),
        P(None, "dp"),
        P("dp"),
    )
    return jax.shard_map(local, mesh=mesh, in_specs=in_specs, out_specs=out_specs, check_vma=False)
```

profile of v0, /device:TPU:0, one launch (start us, length us, event | category | flops | bytes accessed | tf_op | source)
XLA Modules:
  0.0 941.1 jit_solution(3668679954728577496)
XLA Ops:
  16.4 42.3 %all-reduce = bf16[7680]{0:T(1024)(128)(2,1)S(1)} all-reduce(bf16[7680]{0:T(1024)(128)(2,1)S(1)} %dynamic-update-slice), channel_id=1, replica_groups=mesh['dp'=32] {'dp'}, use_global_device_ids=true, to_apply=%add | all-reduce | flops 7680 | bytes 30720
  61.3 40.0 %all-gather = bf16[32,24,2]{1,2,0:T(2,128)(2,1)S(1)} all-gather(bf16[1,24,2]{1,2,0:T(2,128)(2,1)S(1)} %convert_bitcast_fusion), channel_id=1, replica_groups=mesh['dp'=32] {'dp'}, dimensions={0}, use_global_device_ids=true | all-gather | bytes 3168 | tf_op jit(solution)/shard_map/all_gather | solution.py:87
  109.1 9.3 add_convert_fusion.1
  118.4 6.7 copy.80
  125.1 14.5 %fusion.13 = (f32[12,512]{1,0:T(8,128)S(1)}, f32[12,512,1024]{2,1,0:T(8,128)}) fusion(pred[512,1024]{1,0:T(8,128)(4,1)} %get-tuple-element.180, bf16[1024,3,12,64]{0,3,2,1:T(8,128)(2,1)} %bitcast.96), kind=kOutput, calls=%fused_computation.28 | convolution fusion | flops 824174592 | bytes 28073984 | tf_op jit(solution)/shard_map/qhe,khe->hqk/dot_general | solution.py:34
  139.6 12.4 %fusion.1 = f32[12,512]{1,0:T(8,128)S(1)} fusion(f32[12,512]{1,0:T(8,128)S(1)} %get-tuple-element.185, f32[12,512,1024]{2,1,0:T(8,128)} %get-tuple-element.186, pred[512,1024]{1,0:T(8,128)(4,1)} %get-tuple-element.180), kind=kLoop, calls=%fused_computation.13 | loop fusion | flops 25159680 | bytes 25739264 | tf_op jit(solution)/shard_map/reduce_sum | solution.py:117
  155.6 10.1 %fusion.35 = bf16[512,12,64]{0,2,1:T(8,128)(2,1)} fusion(f32[12,512]{1,0:T(8,128)S(1)} %fusion.1, f32[12,512]{1,0:T(8,128)S(1)} %get-tuple-element.185, f32[12,512,1024]{2,1,0:T(8,128)S(1)} %copy-done.1, pred[512,1024]{1,0:T(8,128)(4,1)} %get-tuple-element.180, bf16[1024,3,12,64]{0,3,2,1:T(8,128)(2,1)S(1)} %bitcast.101), kind=kOutput, calls=%fused_computation.80 | convolution fusion | flops 837156864 | bytes 28114944 | tf_op jit(solution)/shard_map/hqk,khe->qhe/dot_general | solution.py:120
  165.7 10.9 %fusion.12 = (f32[12,512]{1,0:T(8,128)S(1)}, f32[12,512,1024]{2,1,0:T(8,128)}) fusion(pred[512,1024]{1,0:T(8,128)(4,1)S(1)} %get-tuple-element.179, bf16[1024,3,12,64]{0,3,2,1:T(8,128)(2,1)S(1)} %bitcast.102), kind=kOutput, calls=%fused_computation.27 | convolution fusion | flops 824174592 | bytes 28073984 | tf_op jit(solution)/shard_map/qhe,khe->hqk/dot_general | solution.py:34
  176.6 13.5 %fusion = f32[12,512]{1,0:T(8,128)} fusion(f32[12,512]{1,0:T(8,128)S(1)} %get-tuple-element.187, f32[12,512,1024]{2,1,0:T(8,128)} %get-tuple-element.188, pred[512,1024]{1,0:T(8,128)(4,1)S(1)} %get-tuple-element.179), kind=kLoop, calls=%fused_computation.12 | loop fusion | flops 25159680 | bytes 25739264 | tf_op jit(solution)/shard_map/reduce_sum | solution.py:117
  192.8 9.7 %fusion.34 = bf16[512,12,64]{0,2,1:T(8,128)(2,1)} fusion(f32[12,512]{1,0:T(8,128)} %fusion, f32[12,512]{1,0:T(8,128)S(1)} %get-tuple-element.187, f32[12,512,1024]{2,1,0:T(8,128)S(1)} %copy-done, pred[512,1024]{1,0:T(8,128)(4,1)S(1)} %get-tuple-element.179, bf16[1024,3,12,64]{0,3,2,1:T(8,128)(2,1)S(1)} %bitcast.103), kind=kOutput, calls=%fused_computation.79 | convolution fusion | flops 837156864 | bytes 28106752 | tf_op jit(solution)/shard_map/hqk,khe->qhe/dot_general | solution.py:120
  210.7 12.9 %multiply_convert_fusion.2 = (bf16[1024,3072]{1,0:T(8,128)(2,1)}, f32[1024,3072]{1,0:T(8,128)}) fusion(f32[3072]{0:T(1024)S(1)} %copy-done.47, bf16[768,3072]{1,0:T(8,128)(2,1)} %all-gather.10.cloned.1.call-done, f32[1024,768]{0,1:T(8,128)S(1)} %get-tuple-element.190, f32[768]{0:T(1024)S(1)} %copy-done.48, f32[768]{0:T(1024)S(1)} %copy-done.39, ...), kind=kOutput, calls=%fused_computation.22 | convolution fusion | flops 4854644736 | bytes 26765312 | tf_op jit(solution)/shard_map/dot_general | solution.py:127
  223.6 39.0 %all-gather.12.cloned.1.call-done = bf16[3072,768]{1,0:T(8,128)(2,1)} async-done(((bf16[96,768]{1,0:T(8,128)(2,1)}), bf16[3072,768]{1,0:T(8,128)(2,1)}) %all-gather.12.cloned.1.call-update) | async-done | bytes 4718608 | tf_op jit(solution)/shard_map/all_gather | solution.py:86
  262.6 9.1 fusion.64
  279.2 15.4 %convert_reduce_fusion = (f32[3072]{0:T(1024)}, bf16[1024,3072]{1,0:T(8,128)(2,1)S(1)}) fusion(bf16[1024,768]{0,1:T(8,128)(2,1)S(1)} %get-tuple-element.165, bf16[3072,768]{1,0:T(8,128)(2,1)S(1)} %bitcast.128, f32[1024,3072]{1,0:T(8,128)} %get-tuple-element.192, f32[3072]{0:T(1024)S(1)} %copy-done.47), kind=kOutput, calls=%fused_computation.18 | convolution fusion | flops 4882166784 | bytes 25190400 | tf_op jit(solution)/shard_map/td,fd->tf/dot_general | solution.py:145
  294.6 7.1 multiply_reduce_fusion.2
  310.4 13.6 %fusion.4 = f32[12,64,1024]{2,1,0:T(8,128)} fusion(bf16[512,12,64]{0,2,1:T(8,128)(2,1)S(1)} %bitcast.113, f32[12,512]{1,0:T(8,128)S(1)} %log_add_fusion, f32[12,512,1024]{2,1,0:T(8,128)} %get-tuple-element.186, pred[512,1024]{1,0:T(8,128)(4,1)S(1)} %copy-done.8), kind=kOutput, calls=%fused_computation.16 | convolution fusion | flops 830472192 | bytes 29646848 | tf_op jit(solution)/shard_map/hqk,qhe->khe/dot_general | solution.py:182
  324.0 20.3 %multiply_reduce_fusion = (f32[12,512]{1,0:T(8,128)S(1)}, f32[12,512,1024]{2,1,0:T(8,128)}) fusion(f32[12,512]{1,0:T(8,128)S(1)} %log_add_fusion, f32[12,512,1024]{2,1,0:T(8,128)} %get-tuple-element.186, pred[512,1024]{1,0:T(8,128)(4,1)S(1)} %copy-done.8, bf16[512,12,64]{0,2,1:T(8,128)(2,1)S(1)} %bitcast.114, bf16[1024,3,12,64]{0,3,2,1:T(8,128)(2,1)} %bitcast.97), kind=kOutput, calls=%fused_computation.1 | convolution fusion | flops 836757504 | bytes 53264384 | tf_op jit(solution)/shard_map/qhe,khe->hqk/dot_general | solution.py:170
  344.2 20.3 %multiply_reduce_fusion.1 = (f32[12,512]{1,0:T(8,128)S(1)}, f32[12,512,1024]{2,1,0:T(8,128)}) fusion(f32[12,512]{1,0:T(8,128)S(1)} %log_add_fusion.1, f32[12,512,1024]{2,1,0:T(8,128)} %get-tuple-element.188, pred[512,1024]{1,0:T(8,128)(4,1)S(1)} %copy-done.6, bf16[512,12,64]{0,2,1:T(8,128)(2,1)S(1)} %bitcast.111, bf16[1024,3,12,64]{0,3,2,1:T(8,128)(2,1)} %bitcast.98), kind=kOutput, calls=%fused_computation.4 | convolution fusion | flops 836757504 | bytes 53264384 | tf_op jit(solution)/shard_map/qhe,khe->hqk/dot_general | solution.py:170
  364.6 42.7 %multiply_convert_fusion = (bf16[12,512,1024]{2,1,0:T(8,128)(2,1)}, bf16[12,512,1024]{2,1,0:T(8,128)(2,1)}) fusion(f32[12,512,1024]{2,1,0:T(8,128)} %get-tuple-element.199, f32[12,512]{1,0:T(8,128)S(1)} %get-tuple-element.198, f32[12,512]{1,0:T(8,128)S(1)} %log_add_fusion, f32[12,512,1024]{2,1,0:T(8,128)} %get-tuple-element.186, ...), kind=kLoop, calls=%fused_computation | loop fusion | flops 75497472 | bytes 126976000 | tf_op jit(solution)/shard_map/convert_element_type | solution.py:174
  407.3 9.5 %fusion.32 = bf16[512,12,64]{0,2,1:T(8,128)(2,1)} fusion(bf16[12,512,1024]{2,1,0:T(8,128)(2,1)} %get-tuple-element.203, bf16[1024,3,12,64]{0,3,2,1:T(8,128)(2,1)S(1)} %bitcast.106), kind=kOutput, calls=%fused_computation.77 | convolution fusion | flops 806092800 | bytes 14942208 | tf_op jit(solution)/shard_map/hqk,khe->qhe/dot_general | solution.py:177
  416.8 8.6 fusion.40
  425.5 9.2 fusion.33
  434.7 7.5 fusion.29
  442.5 12.4 %fusion.26 = bf16[1024,1,12,64]{0,3,2,1:T(8,128)(2,1)S(1)} fusion(f32[12,64,1024]{2,1,0:T(8,128)S(1)} %copy-done.62, bf16[512,12,64]{0,2,1:T(8,128)(2,1)S(1)} %bitcast.112, f32[12,512]{1,0:T(8,128)S(1)} %log_add_fusion.1, f32[12,512,1024]{2,1,0:T(8,128)} %get-tuple-element.188, pred[512,1024]{1,0:T(8,128)(4,1)S(1)} %copy-done.7), kind=kOutput, calls=%fused_computation.73 | convolution fusion | flops 832045056 | bytes 31219712 | tf_op jit(solution)/shard_map/hqk,qhe->khe/dot_general | solution.py:182
  457.8 6.0 fusion.41
  465.6 10.5 %fusion.54 = f32[768,3072]{1,0:T(8,128)} fusion(bf16[1024,3072]{1,0:T(8,128)(2,1)} %copy-done.63, f32[1024,768]{0,1:T(8,128)S(1)} %copy-done.11, f32[768]{0:T(1024)S(1)} %copy-done.49, f32[768]{0:T(1024)S(1)} %copy-done.39, f32[1024]{0:T(1024)S(1)} %fusion.44, f32[1024]{0:T(1024)S(1)} %broadcast_multiply_fusion.1), kind=kOutput, calls=%fused_computation.141 | convolution fusion | flops 4835770368 | bytes 18888704 | tf_op jit(solution)/shard_map/td,tf->df/dot_general | solution.py:149
  477.5 10.5 %fusion.66 = f32[3072,768]{1,0:T(8,128)} fusion(bf16[1024,3072]{1,0:T(8,128)(2,1)} %get-tuple-element.191, bf16[1024,768]{0,1:T(8,128)(2,1)S(1)} %copy-done.24), kind=kOutput, calls=%fused_computation.151 | convolution fusion | flops 4831838208 | bytes 17301504 | tf_op jit(solution)/shard_map/tf,td->fd/dot_general | solution.py:144
  491.6 8.5 multiply_convert_fusion.3
  505.8 40.1 %all-reduce.3 = (f32[2,768]{1,0:T(2,128)S(1)}, f32[7680]{0:T(1024)S(1)}) all-reduce(f32[2,768]{1,0:T(2,128)S(1)} %pad_maximum_fusion.3, f32[7680]{0:T(1024)S(1)} %constant_dynamic-update-slice_fusion), channel_id=6, replica_groups=mesh['dp'=32] {'dp'}, use_global_device_ids=true, to_apply=%region_20.21.clone | all-reduce | flops 9216 | bytes 73728
  548.9 99.7 %reduce-scatter.6.cloned.1.call-done = f32[24,2304]{1,0:T(8,128)} async-done(((f32[768,2304]{1,0:T(8,128)}), f32[24,2304]{1,0:T(8,128)}) %reduce-scatter.6.cloned.1.call-update) | async-done | bytes 221200 | tf_op jit(solution)/shard_map/reduce_scatter | solution.py:210
  650.4 139.4 %reduce-scatter.10.cloned.1.call-done = f32[24,3072]{1,0:T(8,128)} async-done(((f32[768,3072]{1,0:T(8,128)}), f32[24,3072]{1,0:T(8,128)}) %reduce-scatter.10.cloned.1.call-update) | async-done | bytes 294928 | tf_op jit(solution)/shard_map/reduce_scatter | solution.py:212
  791.8 140.1 %reduce-scatter.12.cloned.1.call-done = f32[96,768]{1,0:T(8,128)} async-done(((f32[3072,768]{1,0:T(8,128)}), f32[96,768]{1,0:T(8,128)}) %reduce-scatter.12.cloned.1.call-update) | async-done | bytes 294928 | tf_op jit(solution)/shard_map/reduce_scatter | solution.py:213
  (232 shorter events, 73.9 us)
Async XLA Ops:
  7.2 94.9 %copy-start.17 = (bf16[1024,768]{1,0:T(8,128)(2,1)S(1)}, bf16[1024,768]{1,0:T(8,128)(2,1)}, u32[]{:S(2)}) copy-start(bf16[1024,768]{1,0:T(8,128)(2,1)} %param.27) | copy-start | bytes 4718596
  7.2 96.6 %copy-start.18 = (bf16[1024,768]{1,0:T(8,128)(2,1)S(1)}, bf16[1024,768]{1,0:T(8,128)(2,1)}, u32[]{:S(2)}) copy-start(bf16[1024,768]{1,0:T(8,128)(2,1)} %param.23) | copy-start | bytes 4718596
  7.2 101.9 %all-gather.6.cloned.1.call-start = ((), (), s32[]{:S(2)}) async-start(), calls=%async_computation.4 | async-start | bytes 3649536 | tf_op jit(solution)/shard_map/all_gather | solution.py:83
  9.0 196.1 %all-gather.8.cloned.1.call-start = ((), (), s32[]{:S(2)}) async-start(), calls=%async_computation.5 | async-start | bytes 1216512 | tf_op jit(solution)/shard_map/all_gather | solution.py:84
  10.6 200.0 %all-gather.10.cloned.1.call-start = ((), (), s32[]{:S(2)}) async-start(), calls=%async_computation.6 | async-start | bytes 4866048 | tf_op jit(solution)/shard_map/all_gather | solution.py:85
  12.3 250.3 %all-gather.12.cloned.1.call-start = ((), (), s32[]{:S(2)}) async-start(), calls=%async_computation.7 | async-start | bytes 4866048 | tf_op jit(solution)/shard_map/all_gather | solution.py:86
  14.1 533.3 %reduce-scatter.8.cloned.1.call-start = ((), (), s32[]{:S(2)}) async-start(), calls=%async_computation.9 | async-start | bytes 2433024 | tf_op jit(solution)/shard_map/reduce_scatter | solution.py:211
  15.5 189.7 %copy-start.52 = (f32[1,1024]{1,0:T(1,128)}, f32[1,1024]{1,0:T(1,128)S(1)}, u32[]{:S(2)}) copy-start(f32[1,1024]{1,0:T(1,128)S(1)} %convert_element_type.120) | copy-start | bytes 12292
  109.1 81.0 %copy-start.5 = (pred[512,1024]{1,0:T(8,128)(4,1)}, pred[512,1024]{1,0:T(8,128)(4,1)S(1)}, u32[]{:S(2)}) copy-start(pred[512,1024]{1,0:T(8,128)(4,1)S(1)} %get-tuple-element.179) | copy-start | bytes 1572868
  209.8 91.8 %copy-start.10 = (f32[1024,768]{0,1:T(8,128)}, f32[1024,768]{0,1:T(8,128)S(1)}, u32[]{:S(2)}) copy-start(f32[1024,768]{0,1:T(8,128)S(1)} %get-tuple-element.190) | copy-start | bytes 9437188
  210.7 51.9 %copy-start.50 = (f32[768]{0:T(1024)S(1)}, f32[768]{0:T(1024)}, u32[]{:S(2)}) copy-start(f32[768]{0:T(1024)} %get-tuple-element.174) | copy-start | bytes 9220
  344.2 63.1 %slice-start = ((s8[4718592]{0:T(1024)(128)(4,1)}), s8[524288]{0:T(1024)(128)(4,1)S(1)}, s32[]{:S(2)}) async-start(s8[4718592]{0:T(1024)(128)(4,1)} %bitcast.104), calls=%async_computation.12 | async-start | bytes 1048576
  425.4 223.2 %reduce-scatter.6.cloned.1.call-start = ((), (), s32[]{:S(2)}) async-start(), calls=%async_computation.8 | async-start | bytes 7299072 | tf_op jit(solution)/shard_map/reduce_scatter | solution.py:210
  463.8 326.1 %reduce-scatter.10.cloned.1.call-start = ((), (), s32[]{:S(2)}) async-start(), calls=%async_computation.10 | async-start | bytes 9732096 | tf_op jit(solution)/shard_map/reduce_scatter | solution.py:212
  476.1 455.8 %reduce-scatter.12.cloned.1.call-start = ((), (), s32[]{:S(2)}) async-start(), calls=%async_computation.11 | async-start | bytes 9732096 | tf_op jit(solution)/shard_map/reduce_scatter | solution.py:213
  500.2 45.8 %copy-start.55 = (f32[2,24]{1,0:T(2,128)S(1)}, f32[2,24]{1,0:T(2,128)}, u32[]{:S(2)}) copy-start(f32[2,24]{1,0:T(2,128)} %param.32) | copy-start | bytes 580
  500.2 45.8 %copy-start.56 = (f32[2,24]{1,0:T(2,128)S(1)}, f32[2,24]{1,0:T(2,128)}, u32[]{:S(2)}) copy-start(f32[2,24]{1,0:T(2,128)} %param.44) | copy-start | bytes 580
  500.2 46.4 %copy-start.58 = (f32[240]{0:T(256)S(1)}, f32[240]{0:T(256)}, u32[]{:S(2)}) copy-start(f32[240]{0:T(256)} %param.33) | copy-start | bytes 2884
  500.2 46.4 %copy-start.59 = (f32[240]{0:T(256)S(1)}, f32[240]{0:T(256)}, u32[]{:S(2)}) copy-start(f32[240]{0:T(256)} %param.45) | copy-start | bytes 2884
  500.2 46.4 %copy-start.60 = (f32[240]{0:T(256)S(1)}, f32[240]{0:T(256)}, u32[]{:S(2)}) copy-start(f32[240]{0:T(256)} %param.39) | copy-start | bytes 2884
  500.2 47.1 %copy-start.28 = (f32[24,768]{1,0:T(8,128)S(1)}, f32[24,768]{1,0:T(8,128)}, u32[]{:S(2)}) copy-start(f32[24,768]{1,0:T(8,128)} %param.29) | copy-start | bytes 221188
  500.3 47.0 %copy-start.36 = (f32[24,768]{1,0:T(8,128)S(1)}, f32[24,768]{1,0:T(8,128)}, u32[]{:S(2)}) copy-start(f32[24,768]{1,0:T(8,128)} %param.41) | copy-start | bytes 221188
  500.3 47.0 %copy-start.37 = (f32[24,768]{1,0:T(8,128)S(1)}, f32[24,768]{1,0:T(8,128)}, u32[]{:S(2)}) copy-start(f32[24,768]{1,0:T(8,128)} %param.35) | copy-start | bytes 221188
  500.3 148.3 %copy-start.27 = (f32[24,2304]{1,0:T(8,128)S(1)}, f32[24,2304]{1,0:T(8,128)}, u32[]{:S(2)}) copy-start(f32[24,2304]{1,0:T(8,128)} %param.28) | copy-start | bytes 663556
  500.3 148.3 %copy-start.33 = (f32[24,2304]{1,0:T(8,128)S(1)}, f32[24,2304]{1,0:T(8,128)}, u32[]{:S(2)}) copy-start(f32[24,2304]{1,0:T(8,128)} %param.40) | copy-start | bytes 663556
  500.3 148.3 %copy-start.34 = (f32[24,2304]{1,0:T(8,128)S(1)}, f32[24,2304]{1,0:T(8,128)}, u32[]{:S(2)}) copy-start(f32[24,2304]{1,0:T(8,128)} %param.34) | copy-start | bytes 663556
  503.1 286.7 %copy-start.25 = (f32[24,3072]{1,0:T(8,128)S(1)}, f32[24,3072]{1,0:T(8,128)}, u32[]{:S(2)}) copy-start(f32[24,3072]{1,0:T(8,128)} %param.30) | copy-start | bytes 884740
  503.1 286.7 %copy-start.29 = (f32[24,3072]{1,0:T(8,128)S(1)}, f32[24,3072]{1,0:T(8,128)}, u32[]{:S(2)}) copy-start(f32[24,3072]{1,0:T(8,128)} %param.42) | copy-start | bytes 884740
  503.1 286.7 %copy-start.30 = (f32[24,3072]{1,0:T(8,128)S(1)}, f32[24,3072]{1,0:T(8,128)}, u32[]{:S(2)}) copy-start(f32[24,3072]{1,0:T(8,128)} %param.36) | copy-start | bytes 884740
  503.1 428.8 %copy-start.26 = (f32[96,768]{1,0:T(8,128)S(1)}, f32[96,768]{1,0:T(8,128)}, u32[]{:S(2)}) copy-start(f32[96,768]{1,0:T(8,128)} %param.31) | copy-start | bytes 884740
  503.1 428.8 %copy-start.31 = (f32[96,768]{1,0:T(8,128)S(1)}, f32[96,768]{1,0:T(8,128)}, u32[]{:S(2)}) copy-start(f32[96,768]{1,0:T(8,128)} %param.43) | copy-start | bytes 884740
  503.1 428.8 %copy-start.32 = (f32[96,768]{1,0:T(8,128)S(1)}, f32[96,768]{1,0:T(8,128)}, u32[]{:S(2)}) copy-start(f32[96,768]{1,0:T(8,128)} %param.37) | copy-start | bytes 884740
  (46 other events, 398.5 us)
Sparse Core Ops, SparseCore 0:
  11.5 62.8 all-gather.5
  77.9 52.8 all-gather.7
  134.2 62.5 all-gather.9
  200.2 62.3 all-gather.11
  425.5 97.9 reduce-scatter.7
  530.5 117.9 reduce-scatter.5
  655.1 134.7 reduce-scatter.9
  797.3 134.5 reduce-scatter.11
where the time goes:
time: 952 us; the launch traced here: 941 us
  waiting for transfers between devices  418 us (44%)
  matrix products  245 us (26%)
  blocking collectives  122 us (13%)
  other arithmetic  104 us (11%)
  local copies, waits for them, and re-layouts  35.9 us (4%)
  between operations  15.4 us (2%)
    reduce_scatter x1, waiting for transfers between devices, local(): lax.psum_scatter(grad_reduce, 'dp', scatter_dimension=0, tiled=True)  140 us
    reduce_scatter x1, waiting for transfers between devices, local(): lax.psum_scatter(grad_expand, 'dp', scatter_dimension=0, tiled=True)  139 us
    reduce_scatter x1, waiting for transfers between devices, local(): lax.psum_scatter(grad_qkv, 'dp', scatter_dimension=0, tiled=True)  99.7 us
    unnamed x2, blocking collectives  82.4 us
    convert_element_type x1, other arithmetic, local(): score_grad = (prob_block * (prob_grad - row_dot)).astype(jnp.bfloat16)  42.7 us
    dot_general x2, matrix products, local(): jnp.einsum('qhe,khe->hqk', context_part, values, preferred_element_type=j...  40.6 us
    all_gather x1, blocking collectives, local(): lax.all_gather(norm_gains.astype(jnp.bfloat16), 'dp', axis=1, tiled=True)  40 us
    all_gather x1, waiting for transfers between devices, local(): lax.all_gather(reduce_weight.astype(jnp.bfloat16), 'dp', axis=0, tiled=True)  39 us
  transfers between devices with their start and end apart: 8, of which 4 were waited for; matrix products, arithmetic and copies ran while one was open for 22% of the time, Pallas kernels for 0%

commit v1 on v0

v1 whole, which is shorter than its diff:
```python
import functools
import math

import jax
import jax.numpy as jnp
from jax import lax
from jax.experimental import pallas as pl
from jax.experimental.pallas import tpu as pltpu
from jax.sharding import PartitionSpec as P

D = 768
H = 12
HD = 64
FF = 3072
TOK = 1024
HALF = 512

EPSILON = 1e-05
MASKED = -1000000000.0
rate_matrix = 0.04
rate_proj = 0.5
rate_small = 0.2

f32 = jnp.float32
bf16 = jnp.bfloat16
NN = (((1,), (0,)), ((), ()))
NT = (((1,), (1,)), ((), ()))
TN = (((0,), (0,)), ((), ()))
MESH = pl.DeviceIdType.MESH
VMEM_LIMIT = 60 << 20
IN_VMEM = pl.BlockSpec(memory_space=pltpu.VMEM)
IN_HBM = pl.BlockSpec(memory_space=pl.ANY)
S = jax.ShapeDtypeStruct


def dot(a, b, dims):
    return lax.dot_general(a, b, dims, preferred_element_type=f32)


def lane_half(h, shape):
    return (lax.broadcasted_iota(jnp.int32, shape, 1) // HD) == h


def params(**more):
    return pltpu.CompilerParams(vmem_limit_bytes=VMEM_LIMIT, **more)


class Place:
    def __init__(self):
        me = lax.axis_index("dp")
        self.me = me
        self.c, self.x, self.y, self.z = me % 2, (me // 2) % 2, (me // 4) % 2, me // 8
        self.chip = me // 2
        self.partner = me + 1 - 2 * self.c
        self.xn = me + 2 - 4 * self.x
        self.yn = me + 4 - 8 * self.y
        self.up = me + 8
        self.down = me - 8
        z = self.z
        first = jnp.where(z == 0, 1, jnp.where(z == 1, 0, jnp.where(z == 2, 3, 2)))
        second = jnp.where(z == 0, 2, jnp.where(z == 1, 2, 1))
        third = jnp.where(z < 2, 3, 0)
        self.order = (z, first, second, third)

    def other(self, zz, dx=False, dy=False):
        x = 1 - self.x if dx else self.x
        y = 1 - self.y if dy else self.y
        return zz * 4 + y * 2 + x

    def greet(self):
        barrier = pltpu.get_barrier_semaphore()
        for other in (self.partner, self.xn, self.yn):
            pl.semaphore_signal(barrier, inc=1, device_id=(other,), device_id_type=MESH)

        @pl.when(self.z < 3)
        def _():
            pl.semaphore_signal(barrier, inc=1, device_id=(self.up,), device_id_type=MESH)

        @pl.when(self.z > 0)
        def _():
            pl.semaphore_signal(barrier, inc=1, device_id=(self.down,), device_id_type=MESH)

        ends = jnp.where((self.z == 0) | (self.z == 3), 4, 5)
        pl.semaphore_wait(barrier, ends)


def remote(src, dst, send, recv, other):
    return pltpu.make_async_remote_copy(
        src_ref=src, dst_ref=dst, send_sem=send, recv_sem=recv, device_id=(other,), device_id_type=MESH
    )


def arrived(view, sem):
    pltpu.make_async_copy(view, view, sem).wait()


DMA = pltpu.SemaphoreType.DMA


class Gather:
    def __init__(self, place, shard, full, scratch):
        self.p = place
        self.shard = shard
        self.full = full
        self.rows = 2 * shard.shape[0]
        self.half = shard.shape[1] // 2
        self.stage, self.own, self.ls, self.zs, self.zr, self.xs, self.xr, self.ys, self.yr, self.hs, self.hr, self.ps, self.pr = scratch

    @staticmethod
    def scratch(rows, cols, dtype):
        return [pltpu.VMEM((2 * rows, cols), f32), pltpu.VMEM((2 * rows, cols), dtype), DMA((4,)), DMA((5,))] + [DMA((4,))] * 9

    def cut(self, c):
        return pl.ds(pl.multiple_of(c * self.half, 128), self.half)

    def at(self, chip, count=1):
        start = pl.multiple_of(chip * self.rows, 16)
        return self.full.at[pl.ds(start, count * self.rows), self.cut(self.p.c)]

    def loads(self):
        p = self.p
        mine = self.stage.at[pl.ds(pl.multiple_of(p.c * (self.rows // 2), 8), self.rows // 2)]
        return pltpu.make_async_copy(self.shard, mine, self.ls.at[0]), remote(self.shard, mine, self.ls.at[1], self.ls.at[2], p.partner)

    def keep(self):
        return pltpu.make_async_copy(self.own.at[:, self.cut(self.p.c)], self.at(self.p.chip), self.ls.at[3])

    def along_z(self, k):
        p = self.p
        zz = p.order[k]
        view = self.at(p.other(zz))
        src = view if k else self.own.at[:, self.cut(p.c)]
        up = remote(src, view, self.zs.at[k], self.zr.at[zz], p.up)
        if k == 0:
            down = remote(src, view, self.zs.at[4], self.zr.at[zz], p.down)
            return (p.z < 3, up), (p.z > 0, down)
        down = remote(src, view, self.zs.at[k], self.zr.at[zz], p.down)
        return ((p.z < 3) & (zz < p.z), up), ((p.z > 0) & (zz > p.z), down)

    def across(self, k):
        p = self.p
        zz = p.order[k]
        view = self.at(p.other(zz))
        src = view if k else self.own.at[:, self.cut(p.c)]
        return (
            remote(src, view, self.xs.at[zz], self.xr.at[zz], p.xn),
            remote(src, view, self.ys.at[zz], self.yr.at[zz], p.yn),
        )

    def onward(self, k):
        p = self.p
        zz = p.order[k]
        even = k % 2 == 0
        view = self.at(p.other(zz, dx=even, dy=not even))
        return remote(view, view, self.hs.at[zz], self.hr.at[zz], p.yn if even else p.xn)

    def to_partner(self, k):
        zz = self.p.order[k]
        view = self.at(4 * zz, 4)
        return remote(view, view, self.ps.at[zz], self.pr.at[zz], self.p.partner)

    def load(self):
        for copy in self.loads():
            copy.start()

    def begin(self):
        local, pair = self.loads()
        local.wait()
        pair.wait_recv()
        self.own[...] = self.stage[...].astype(self.own.dtype)
        for cond, copy in self.along_z(0):
            pl.when(cond)(copy.start)
        for copy in self.across(0):
            copy.start()
        self.keep().start()

    def column(self, k):
        zz = self.p.order[k]
        arrived(self.at(self.p.other(zz)), self.zr.at[zz])
        for cond, copy in self.along_z(k):
            pl.when(cond)(copy.start)
        for copy in self.across(k):
            copy.start()

    def plane(self, k):
        p = self.p
        zz = p.order[k]
        even = k % 2 == 0
        arrived(self.at(p.other(zz, dx=even, dy=not even)), (self.xr if even else self.yr).at[zz])
        self.onward(k).start()

    def corner(self, k):
        p = self.p
        zz = p.order[k]
        even = k % 2 == 0
        arrived(self.at(p.other(zz, dx=not even, dy=even)), (self.yr if even else self.xr).at[zz])
        arrived(self.at(p.other(zz, True, True)), self.hr.at[zz])
        if k == 0:
            self.keep().wait()
        self.to_partner(k).start()

    def step(self, s):
        if s == 0:
            self.begin()
        if 1 <= s <= 3:
            self.column(s)
        if 1 <= s <= 4:
            self.plane(s - 1)
        if 2 <= s <= 5:
            self.corner(s - 2)
        if s == 6:
            self.finish()

    def finish(self):
        p = self.p
        for zz in range(4):
            start = pl.multiple_of(4 * zz * self.rows, 16)
            arrived(self.full.at[pl.ds(start, 4 * self.rows), self.cut(1 - p.c)], self.pr.at[zz])
        self.loads()[1].wait_send()
        for k in range(4):
            for cond, copy in self.along_z(k):
                pl.when(cond)(copy.wait_send)
            for copy in self.across(k):
                copy.wait_send()
            self.onward(k).wait_send()
            self.to_partner(k).wait_send()


GATHER_SCRATCH = 13


def gather_kernel(count, *refs):
    shards, fulls, rest = refs[:count], refs[count : 2 * count], refs[2 * count :]
    place = Place()
    place.greet()
    jobs = [Gather(place, shards[i], fulls[i], rest[i * GATHER_SCRATCH : (i + 1) * GATHER_SCRATCH]) for i in range(count)]
    for job in jobs:
        job.load()
    for t in range(count + 6):
        for i, job in enumerate(jobs):
            if 0 <= t - i <= 6:
                job.step(t - i)


def gather_all(shards, dtypes):
    count = len(shards)
    return pl.pallas_call(
        functools.partial(gather_kernel, count),
        in_specs=[IN_HBM] * count,
        out_specs=[IN_HBM] * count,
        out_shape=[S((32 * s.shape[0], s.shape[1]), d) for s, d in zip(shards, dtypes)],
        scratch_shapes=sum([Gather.scratch(*s.shape, d) for s, d in zip(shards, dtypes)], []),
        compiler_params=params(collective_id=0, has_side_effects=True),
        name="gather",
    )(*shards)


class Scatter:
    def __init__(self, place, grad, out, scratch):
        self.p = place
        self.grad = grad
        self.out = out
        self.rows = 2 * out.shape[0]
        self.half = out.shape[1] // 2
        self.bp, self.bh, self.bx, self.by, self.bz, self.fin = scratch[:6]
        self.ps, self.pr, self.hs, self.hr, self.xs, self.xr, self.ys, self.yr, self.zs, self.zr, self.fs = scratch[6:]

    @staticmethod
    def scratch(rows, cols, dtype):
        rows, half = 2 * rows, cols // 2
        bufs = [pltpu.VMEM((n * rows, half), dtype) for n in (16, 4, 4, 4, 5)]
        return bufs + [pltpu.VMEM((rows, half), f32)] + [DMA((4,))] * 9 + [DMA((5,)), DMA((3,))]

    def cut(self, c):
        return pl.ds(pl.multiple_of(c * self.half, 128), self.half)

    def span(self, n, count=1):
        return pl.ds(pl.multiple_of(n * self.rows, 16), count * self.rows)

    def at(self, chip):
        return self.grad.at[self.span(chip), self.cut(self.p.c)]

    def slot(self, buf, n):
        return buf.at[self.span(n)]

    def add(self, view, *terms):
        total = view[...].astype(f32)
        for term in terms:
            total = total + term[...].astype(f32)
        view[...] = total.astype(view.dtype)

    def to_partner(self, zz):
        p = self.p
        src = self.grad.at[self.span(4 * zz, 4), self.cut(1 - p.c)]
        return remote(src, self.bp.at[self.span(4 * zz, 4)], self.ps.at[zz], self.pr.at[zz], p.partner)

    def corner(self, k):
        p = self.p
        zz = p.order[k]
        return remote(self.at(p.other(zz, True, True)), self.slot(self.bh, zz), self.hs.at[zz], self.hr.at[zz], p.xn if k % 2 else p.yn)

    def side(self, k, along_x):
        p = self.p
        zz = p.order[k]
        src = self.at(p.other(zz, dx=along_x, dy=not along_x))
        if along_x:
            return remote(src, self.slot(self.bx, zz), self.xs.at[zz], self.xr.at[zz], p.xn)
        return remote(src, self.slot(self.by, zz), self.ys.at[zz], self.yr.at[zz], p.yn)

    def chain(self, k):
        p = self.p
        zz = p.order[k]
        src = self.at(p.other(zz))
        up = remote(src, self.slot(self.bz, zz), self.zs.at[k], self.zr.at[zz], p.up)
        place = jnp.where(zz == p.z - 1, 4, zz)
        down = remote(src, self.slot(self.bz, place), self.zs.at[k], self.zr.at[place], p.down)
        return (zz > p.z, up), (zz < p.z, down)

    def last(self):
        p = self.p
        rows = self.rows // 2
        part = lambda c: self.fin.at[pl.ds(pl.multiple_of(c * rows, 8), rows)]
        dst = self.out.at[:, self.cut(p.c)]
        return pltpu.make_async_copy(part(p.c), dst, self.fs.at[0]), remote(part(1 - p.c), dst, self.fs.at[1], self.fs.at[2], p.partner)

    def step(self, s):
        if s == 0:
            for k in (3, 2, 1, 0):
                self.to_partner(self.p.order[k]).start()
        if 1 <= s <= 4:
            self.pair(4 - s)
        if 2 <= s <= 5:
            self.side_on(5 - s)
        if 3 <= s <= 5:
            self.column(6 - s)
        if s == 6:
            self.total()
        if s == 7:
            self.finish()

    def pair(self, k):
        p = self.p
        zz = p.order[k]
        self.to_partner(zz).wait_recv()

        @pl.loop(0, 4)
        def _(j):
            chip = 4 * zz + j
            self.add(self.at(chip), self.slot(self.bp, chip))

        self.corner(k).start()
        self.side(k, along_x=k % 2 == 1).start()

    def side_on(self, k):
        p = self.p
        zz = p.order[k]
        even = k % 2 == 0
        self.corner(k).wait_recv()
        self.add(self.at(p.other(zz, dx=even, dy=not even)), self.slot(self.bh, zz))
        self.side(k, along_x=even).start()

    def gathered(self, k):
        zz = self.p.order[k]
        self.side(k, True).wait_recv()
        self.side(k, False).wait_recv()
        self.add(self.at(self.p.other(zz)), self.slot(self.bx, zz), self.slot(self.by, zz))

    def column(self, k):
        p = self.p
        zz = p.order[k]
        self.gathered(k)

        @pl.when(((zz > p.z) & (p.z > 0)) | ((zz < p.z) & (p.z < 3)))
        def _():
            arrived(self.slot(self.bz, zz), self.zr.at[zz])
            self.add(self.at(p.other(zz)), self.slot(self.bz, zz))

        for cond, copy in self.chain(k):
            pl.when(cond)(copy.start)

    def total(self):
        p = self.p
        self.gathered(0)
        self.fin[...] = self.at(p.chip)[...].astype(f32)

        @pl.when(p.z > 0)
        def _():
            arrived(self.slot(self.bz, p.z), self.zr.at[p.z])
            self.fin[...] += self.slot(self.bz, p.z)[...].astype(f32)

        @pl.when(p.z < 3)
        def _():
            arrived(self.slot(self.bz, 4), self.zr.at[4])
            self.fin[...] += self.slot(self.bz, 4)[...].astype(f32)

        for copy in self.last():
            copy.start()

    def finish(self):
        p = self.p
        for k in range(4):
            self.to_partner(p.order[k]).wait_send()
            self.corner(k).wait_send()
            self.side(k, True).wait_send()
            self.side(k, False).wait_send()
            if k:
                for cond, copy in self.chain(k):
                    pl.when(cond)(copy.wait_send)
        local, pair = self.last()
        local.wait()
        pair.wait_send()
        arrived(self.out.at[:, self.cut(1 - p.c)], self.fs.at[2])


SCATTER_SCRATCH = 17


def scatter_kernel(count, *refs):
    inputs, outs, rest = refs[:count], refs[count : 2 * count], refs[2 * count :]
    place = Place()
    place.greet()
    each = SCATTER_SCRATCH + 2
    jobs, loads = [], []
    for i in range(count):
        held, load, *own = rest[i * each : (i + 1) * each]
        jobs.append(Scatter(place, held, outs[i], own))
        loads.append(pltpu.make_async_copy(inputs[i], held, load))
        loads[-1].start()
    for t in range(count + 7):
        for i, job in enumerate(jobs):
            s = t - i
            if s == 0:
                loads[i].wait()
            if 0 <= s <= 7:
                job.step(s)


def scatter_all(grads):
    count = len(grads)
    scratch = []
    for g in grads:
        scratch += [pltpu.VMEM(g.shape, g.dtype), DMA(())]
        scratch += Scatter.scratch(g.shape[0] // 32, g.shape[1], g.dtype)
    return pl.pallas_call(
        functools.partial(scatter_kernel, count),
        in_specs=[IN_HBM] * count,
        out_specs=[IN_VMEM] * count,
        out_shape=[S((g.shape[0] // 32, g.shape[1]), f32) for g in grads],
        scratch_shapes=scratch,
        compiler_params=params(collective_id=1, has_side_effects=True),
        name="scatter",
    )(*grads)


def rotation(segments):
    counts = [jnp.sum((segments == u).astype(jnp.int32)) for u in range(3)]
    before, start = jnp.int32(0), jnp.int32(0)
    taken = jnp.bool_(False)
    for u in range(4):
        here = (counts[u] == HALF) & ~taken if u < 3 else ~taken
        start = jnp.where(here, before, start)
        taken = taken | here
        if u < 3:
            before = before + counts[u]
    return start


def column_of(row):
    return jnp.broadcast_to(row, (128, row.shape[1])).T


def entry_kernel(feat_ref, pos_ref, cot_ref, seg_ref, valid_ref, start_ref, entry_ref, low_ref, cot_out_ref, bias_ref, valid_out_ref):
    back = lax.rem(TOK - start_ref[0], TOK)
    valid = valid_ref[...].astype(f32)
    seg = seg_ref[...].astype(f32)
    entry = (feat_ref[...].astype(f32) + pos_ref[...].astype(f32)) * column_of(valid)[:, :1]
    entry = pltpu.roll(entry, back, 0)
    entry_ref[...] = entry
    low_ref[...] = entry.astype(bf16)
    cot_out_ref[...] = pltpu.roll(cot_ref[...], back, 0)
    valid = pltpu.roll(jnp.broadcast_to(valid, (8, TOK)), back, 1)[:1]
    seg = pltpu.roll(jnp.broadcast_to(seg, (8, TOK)), back, 1)[:1]
    valid_out_ref[...] = column_of(valid)
    for h in range(2):
        part = slice(h * HALF, (h + 1) * HALF)
        seg_col = column_of(seg[:, part])[:, :1]
        same = seg_col == seg[:, part]
        rows = lax.broadcasted_iota(jnp.int32, (HALF, HALF), 0)
        cols = lax.broadcasted_iota(jnp.int32, (HALF, HALF), 1)
        allowed = same & ((valid[:, part] > 0.0) | (rows == cols))
        bias_ref[h] = jnp.where(allowed, 0.0, MASKED)


def qkv_kernel(low_ref, weight_ref, bias_ref, out_ref):
    for k in range(3):
        part = slice(k * D, (k + 1) * D)
        out_ref[:, part] = (dot(low_ref[...], weight_ref[:, part], NN) + bias_ref[:, part]).astype(bf16)


def attend_kernel(q_ref, k_ref, v_ref, bias_ref, out_ref, prob_ref):
    q, k, v = q_ref[...] * jnp.bfloat16(0.125), k_ref[...], v_ref[...]
    outs = []
    for h in range(2):
        qh = jnp.where(lane_half(h, q.shape), q, jnp.bfloat16(0))
        scores = dot(qh, k, NT) + bias_ref[0]
        scores = jnp.exp(scores - jnp.max(scores, 1, keepdims=True))
        probs = (scores * (1.0 / jnp.sum(scores, 1, keepdims=True))).astype(bf16)
        prob_ref[h] = probs
        outs.append(dot(probs, v, NN))
    out_ref[...] = jnp.where(lane_half(0, outs[0].shape), outs[0], outs[1]).astype(bf16)


def attend_back_kernel(q_ref, k_ref, v_ref, grad_ref, ctx_ref, prob_ref, dq_ref, dk_ref, dv_ref):
    q, k, v, grad = q_ref[...], k_ref[...], v_ref[...], grad_ref[...]
    product = grad.astype(f32) * ctx_ref[...].astype(f32)
    dq, dk, dv = [], [], []
    for h in range(2):
        lanes = lane_half(h, grad.shape)
        grad_h = jnp.where(lanes, grad, jnp.bfloat16(0))
        row_dot = jnp.sum(jnp.where(lanes, product, 0.0), 1, keepdims=True)
        probs = prob_ref[h]
        ds = (probs.astype(f32) * (dot(grad_h, v, NT) - row_dot)).astype(bf16)
        dq.append(dot(ds, k, NN))
        dk.append(dot(ds, q, TN))
        dv.append(dot(probs, grad, TN))
    lanes = lane_half(0, grad.shape)
    dq_ref[...] = (jnp.where(lanes, dq[0], dq[1]) * 0.125).astype(bf16)
    dk_ref[...] = (jnp.where(lanes, dk[0], dk[1]) * 0.125).astype(bf16)
    dv_ref[...] = jnp.where(lanes, dv[0], dv[1]).astype(bf16)


def pair_block(offset):
    return pl.BlockSpec((HALF, 2 * HD), lambda i, j: (i, offset + j))


PROBS = pl.BlockSpec((2, HALF, HALF), lambda i, j: (i * (H // 2) + j, 0, 0))


def attend(qkv, bias):
    return pl.pallas_call(
        attend_kernel,
        grid=(2, H // 2),
        in_specs=[pair_block(0), pair_block(H // 2), pair_block(H), pl.BlockSpec((1, HALF, HALF), lambda i, j: (i, 0, 0))],
        out_specs=[pair_block(0), PROBS],
        out_shape=[S((TOK, D), bf16), S((2 * H, HALF, HALF), bf16)],
        compiler_params=params(),
        name="attend",
    )(qkv, qkv, qkv, bias)


def attend_back(qkv, grad, ctx, probs):
    return pl.pallas_call(
        attend_back_kernel,
        grid=(2, H // 2),
        in_specs=[pair_block(0), pair_block(H // 2), pair_block(H), pair_block(0), pair_block(0), PROBS],
        out_specs=[pair_block(0)] * 3,
        out_shape=[S((TOK, D), bf16)] * 3,
        compiler_params=params(),
        name="attend_back",
    )(qkv, qkv, qkv, grad, ctx, probs)


ROWS = 256
COLS = 768


def normed_of(residual):
    center = residual - jnp.mean(residual, 1, keepdims=True)
    scale = lax.rsqrt(jnp.mean(center * center, 1, keepdims=True) + EPSILON)
    return center * scale, scale


def norm_back(grad, gain, unit, scale):
    grad = grad * gain
    return scale * (grad - jnp.mean(grad, 1, keepdims=True) - unit * jnp.mean(grad * unit, 1, keepdims=True))


def ffn_kernel(
    ctx_ref, entry_ref, cot_ref, proj_ref, expand_ref, reduce_ref, vec_ref, b1_ref,
    out_ref, first_ref, gctx_ref, dproj_ref, dexpand_ref, dreduce_ref, dvec_ref, db1_ref,
    low_ref, act_ref, gffn_ref, gpre_ref, gbranch_ref, pre_ref, cdf_ref,
):
    dvec_ref[...] = jnp.zeros_like(dvec_ref)
    db1_ref[...] = jnp.zeros_like(db1_ref)
    b_o, b_2, g_1, g_2, c_1, c_2 = [vec_ref[i : i + 1, :] for i in range(6)]

    @pl.loop(0, TOK // ROWS)
    def _(t):
        rows = pl.ds(pl.multiple_of(t * ROWS, ROWS), ROWS)
        unit_1, scale_1 = normed_of(entry_ref[rows, :] + dot(ctx_ref[rows, :], proj_ref[...], NN) + b_o)
        normed = unit_1 * g_1 + c_1
        low = normed.astype(bf16)
        low_ref[rows, :] = low
        total = normed + b_2
        for k in range(FF // COLS):
            cols = slice(k * COLS, (k + 1) * COLS)
            pre = dot(low, expand_ref[:, cols], NN) + b1_ref[:, cols]
            cdf = 0.5 + 0.5 * lax.erf(pre * 0.7071067811865476)
            pre_ref[:, cols] = pre
            cdf_ref[:, cols] = cdf
            act = (pre * cdf).astype(bf16)
            act_ref[rows, cols] = act
            total = total + dot(act, reduce_ref[cols, :], NN)
        unit_2, scale_2 = normed_of(total)
        out_ref[rows, :] = (unit_2 * g_2 + c_2).astype(bf16)
        grad = cot_ref[rows, :].astype(f32)
        dvec_ref[3:4, :] += jnp.sum(grad * unit_2, 0, keepdims=True)
        dvec_ref[5:6, :] += jnp.sum(grad, 0, keepdims=True)
        total = norm_back(grad, g_2, unit_2, scale_2)
        gffn = total.astype(bf16)
        gffn_ref[rows, :] = gffn
        dvec_ref[1:2, :] += jnp.sum(gffn.astype(f32), 0, keepdims=True)
        for k in range(FF // COLS):
            cols = slice(k * COLS, (k + 1) * COLS)
            pre = pre_ref[:, cols]
            slope = cdf_ref[:, cols] + pre * (0.3989422804014327 * jnp.exp(-0.5 * pre * pre))
            gpre = (dot(gffn, reduce_ref[cols, :], NT) * slope).astype(bf16)
            gpre_ref[rows, cols] = gpre
            db1_ref[:, cols] += jnp.sum(gpre.astype(f32), 0, keepdims=True)
            total = total + dot(gpre, expand_ref[:, cols], NT)
        dvec_ref[2:3, :] += jnp.sum(total * unit_1, 0, keepdims=True)
        dvec_ref[4:5, :] += jnp.sum(total, 0, keepdims=True)
        first = norm_back(total, g_1, unit_1, scale_1)
        first_ref[rows, :] = first
        branch = first.astype(bf16)
        gbranch_ref[rows, :] = branch
        dvec_ref[0:1, :] += jnp.sum(branch.astype(f32), 0, keepdims=True)
        gctx_ref[rows, :] = dot(branch, proj_ref[...], NT).astype(bf16)

    @pl.loop(0, FF // 256)
    def _(t):
        part = pl.ds(pl.multiple_of(t * 256, 256), 256)
        dreduce_ref[part, :] = dot(act_ref[:, part], gffn_ref[...], TN).astype(bf16)
        dexpand_ref[:, part] = dot(low_ref[...], gpre_ref[:, part], TN).astype(bf16)

    @pl.loop(0, D // 256)
    def _(t):
        part = pl.ds(pl.multiple_of(t * 256, 256), 256)
        dproj_ref[part, :] = dot(ctx_ref[:, part], gbranch_ref[...], TN).astype(bf16)


def ffn(*arrays):
    return pl.pallas_call(
        ffn_kernel,
        in_specs=[IN_VMEM] * 8,
        out_specs=[IN_VMEM] * 8,
        out_shape=[
            S((TOK, D), bf16), S((TOK, D), f32), S((TOK, D), bf16), S((D, D), bf16),
            S((D, FF), bf16), S((FF, D), bf16), S((8, D), f32), S((1, FF), f32),
        ],
        scratch_shapes=[
            pltpu.VMEM((TOK, D), bf16), pltpu.VMEM((TOK, FF), bf16), pltpu.VMEM((TOK, D), bf16), pltpu.VMEM((TOK, FF), bf16),
            pltpu.VMEM((TOK, D), bf16), pltpu.VMEM((ROWS, FF), f32), pltpu.VMEM((ROWS, FF), f32),
        ],
        compiler_params=pltpu.CompilerParams(vmem_limit_bytes=62 << 20),
        name="ffn",
    )(*arrays)


def tail_kernel(low_ref, dq_ref, dk_ref, dv_ref, weight_ref, first_ref, valid_ref, out_ref, start_ref, grad_ref, input_ref, layer_ref, sums_ref):
    total = first_ref[...]
    for k, part_ref in enumerate((dq_ref, dk_ref, dv_ref)):
        part = slice(k * D, (k + 1) * D)
        grad_ref[:, part] = dot(low_ref[...], part_ref[...], TN).astype(bf16)
        total = total + dot(part_ref[...], weight_ref[:, part], NT)
        sums_ref[k : k + 1, :] = jnp.sum(part_ref[...].astype(f32), 0, keepdims=True)
    total = (total * valid_ref[:, :1]).astype(bf16)
    input_ref[...] = pltpu.roll(total, start_ref[0], 0)
    layer_ref[...] = pltpu.roll(out_ref[...], start_ref[0], 0)


def update_kernel(rates, *refs):
    for i, rate in enumerate(rates):
        w_ref, g_ref, m_ref, a_ref = refs[4 * i : 4 * i + 4]
        outs = refs[4 * len(rates) + 4 * i : 4 * len(rates) + 4 * i + 4]
        grad = g_ref[...]
        velocity = 0.5 * m_ref[...] + grad
        master = w_ref[...] - rate * (grad + 0.5 * velocity)
        for ref, value in zip(outs, (grad, master, velocity, 0.5 * a_ref[...] + 0.5 * master)):
            ref[...] = value


def update(rates, arrays):
    return pl.pallas_call(
        functools.partial(update_kernel, rates),
        in_specs=[IN_VMEM] * len(arrays),
        out_specs=[IN_VMEM] * len(arrays),
        out_shape=[S(a.shape, f32) for a in arrays],
        compiler_params=params(),
        name="update",
    )(*arrays)


def whole(kernel, name, shapes, *arrays, scalars=()):
    return pl.pallas_call(
        kernel,
        in_specs=[IN_VMEM] * len(arrays) + [pl.BlockSpec(memory_space=pltpu.SMEM)] * len(scalars),
        out_specs=[IN_VMEM] * len(shapes),
        out_shape=[S(*s) for s in shapes],
        compiler_params=params(),
        name=name,
    )(*arrays, *scalars)


def rounded(x):
    return lax.reduce_precision(x, 8, 7)


def packed(bias_rows, gain_rows):
    n = bias_rows.shape[0]
    rows = jnp.stack([jnp.pad(r, ((0, 0), (0, 256 - r.shape[1]))) for r in (bias_rows, gain_rows)], axis=1)
    return jnp.pad(rows, ((0, 0), (0, 6), (0, 0))).reshape(8 * n, 256)


def local(linked, *args):
    (
        features, pos_conv, segment_ids, frame_valid, cotangent,
        qkv_weight, proj_weight, expand_weight, reduce_weight, norm_gains, bias_vector,
        qkv_moment, proj_moment, expand_moment, reduce_moment, gains_moment, bias_moment,
        qkv_average, proj_average, expand_average, reduce_average, gains_average, bias_average,
    ) = args
    ranks = lax.axis_size("dp")
    bias_len = bias_vector.shape[0]
    gain_len = norm_gains.shape[1]
    shards = [qkv_weight, proj_weight, expand_weight, reduce_weight]
    small = packed(rounded(bias_vector)[None], rounded(norm_gains).reshape(1, -1))
    if linked:
        small_full, qkv_full, proj_full, expand_full, reduce_full = gather_all([small] + shards, [f32] + [bf16] * 4)
    else:
        small_full, qkv_full, proj_full, expand_full, reduce_full = [
            lax.all_gather(s, "dp", axis=0, tiled=True) for s in [small] + [w.astype(bf16) for w in shards]
        ]
    small_full = small_full.reshape(ranks, 8, 256)
    bias_full = small_full[:, 0, :bias_len].reshape(-1)
    gains_full = small_full[:, 1, : 2 * gain_len].reshape(ranks, 2, gain_len).transpose(1, 0, 2).reshape(2, D)
    start = rotation(segment_ids)[None]
    entry, entry_low, cot, mask, valid = whole(
        entry_kernel,
        "entry",
        [((TOK, D), f32), ((TOK, D), bf16), ((TOK, D), bf16), ((2, HALF, HALF), f32), ((TOK, 128), f32)],
        features, pos_conv, cotangent, segment_ids, frame_valid, scalars=(start,),
    )
    qkv_bias = jnp.concatenate([bias_full[:D], jnp.zeros((D,), f32), bias_full[D : 2 * D]])[None]
    (qkv,) = whole(qkv_kernel, "qkv", [((TOK, 3 * D), bf16)], entry_low, qkv_full, qkv_bias)
    ctx, probs = attend(qkv, mask)
    vectors = jnp.concatenate(
        [
            bias_full[2 * D : 3 * D][None], bias_full[3 * D + FF : 4 * D + FF][None], gains_full,
            bias_full[4 * D + FF :].reshape(2, D), jnp.zeros((2, D), f32),
        ]
    )
    layer, first, grad_ctx, proj_part, expand_part, reduce_part, dvec, db1 = ffn(
        ctx, entry, cot, proj_full, expand_full, reduce_full, vectors, bias_full[3 * D : 3 * D + FF][None]
    )
    dq, dk, dv = attend_back(qkv, grad_ctx, ctx, probs)
    qkv_part, grad_input, layer_out, sums = whole(
        tail_kernel,
        "tail",
        [((D, 3 * D), bf16), ((TOK, D), bf16), ((TOK, D), bf16), ((8, D), f32)],
        entry_low, dq, dk, dv, qkv_full, first, valid, layer, scalars=(start,),
    )
    bias_part = jnp.concatenate([sums[0], sums[2], dvec[0], db1[0], dvec[1], dvec[4], dvec[5]]).reshape(ranks, bias_len)
    gain_part = dvec[2:4].reshape(2, ranks, gain_len).transpose(1, 0, 2).reshape(ranks, 2 * gain_len)
    parts = [reduce_part, expand_part, proj_part, qkv_part, packed(bias_part, gain_part)]
    if linked:
        parts = scatter_all(parts)
    else:
        parts = [lax.psum_scatter(p.astype(f32), "dp", scatter_dimension=0, tiled=True) for p in parts]
    reduce_grad, expand_grad, proj_grad, qkv_grad, small_grad = parts
    root = math.sqrt(ranks * features.shape[0])
    matrix, proj, little = rate_matrix / root, rate_proj / root, rate_small / root
    updated = update(
        (matrix, proj, matrix, matrix),
        [
            qkv_weight, qkv_grad, qkv_moment, qkv_average,
            proj_weight, proj_grad, proj_moment, proj_average,
            expand_weight, expand_grad, expand_moment, expand_average,
            reduce_weight, reduce_grad, reduce_moment, reduce_average,
        ],
    )

    def nesterov(master, gradient, moment, average):
        velocity = 0.5 * moment + gradient
        renewed = master - little * (gradient + 0.5 * velocity)
        return gradient, renewed, velocity, 0.5 * average + 0.5 * renewed

    gains_new = nesterov(norm_gains, small_grad[1, : 2 * gain_len].reshape(2, gain_len), gains_moment, gains_average)
    bias_new = nesterov(bias_vector, small_grad[0, :bias_len], bias_moment, bias_average)
    results = [layer_out, grad_input]
    for i in range(4):
        results += [updated[i], updated[4 + i], updated[8 + i], updated[12 + i], gains_new[i], bias_new[i]]
    return tuple(results)


def solution(mesh):
    linked = mesh.shape["dp"] == 32
    rows, lanes, line = P("dp", None), P(None, "dp"), P("dp")
    six = (rows, rows, rows, rows, lanes, line)
    return jax.shard_map(
        functools.partial(local, linked),
        mesh=mesh,
        in_specs=(rows,) * 5 + six * 3,
        out_specs=(rows, rows) + six * 4,
        check_vma=False,
    )
```

time: 952 us -> 311 us (0.33); the launches traced: 941 us -> 311 us
  waiting for transfers between devices: 418 us -> 0 us
  Pallas kernels: 0 us -> 294 us
  matrix products: 245 us -> 0 us
  blocking collectives: 122 us -> 0 us
  other arithmetic: 104 us -> 3.15 us
  local copies, waits for them, and re-layouts: 35.9 us -> 7.82 us
  between operations: 15.4 us -> 5.53 us
    reduce_scatter x4 -> x0, waiting for transfers between devices: 379 us -> none  [the longest x1 140 us: local(): lax.psum_scatter(grad_reduce, 'dp', scatter_dimension=0, tiled=True)]
    pallas_call x0 -> x9, Pallas kernels: none -> 294 us  [the longest x1 83.4 us: scatter_all(): pl.pallas_call(functools.partial(scatter_kernel, count), in_specs=[IN_HBM...]
    dot_general x24 -> x0, matrix products: 245 us -> none  [the longest x2 40.6 us: local(): jnp.einsum('qhe,khe->hqk', context_part, values, preferred_element_type=j...]
    unnamed x2 -> x0, blocking collectives: 82.4 us -> none
    convert_element_type x7 -> x0, other arithmetic: 50.6 us -> none  [the longest x1 42.7 us: local(): score_grad = (prob_block * (prob_grad - row_dot)).astype(jnp.bfloat16)]
    all_gather x1 -> x0, blocking collectives: 40 us -> none  [local(): lax.all_gather(norm_gains.astype(jnp.bfloat16), 'dp', axis=1, tiled=True)]
    all_gather x4 -> x0, waiting for transfers between devices: 39 us -> none  [the longest x1 39 us: local(): lax.all_gather(reduce_weight.astype(jnp.bfloat16), 'dp', axis=0, tiled=True)]
    reduce_sum x9 -> x1, other arithmetic: 38 us -> 1.37 us  [rotation(): counts = [jnp.sum((segments == u).astype(jnp.int32)) for u in range(3)]]
  transfers between devices with their start and end apart: 8 -> 0, of which waited for: 4 -> 0; matrix products, arithmetic and copies ran while one was open for 22% -> 0% of each run, Pallas kernels for 0% -> 0%
where the time goes in v1:
time: 311 us
  Pallas kernels  294 us (95%)
  local copies, waits for them, and re-layouts  7.82 us (3%)
  between operations  5.53 us (2%)
  other arithmetic  3.15 us (1%)
    pallas_call x1, Pallas kernels, scatter_all(): pl.pallas_call(functools.partial(scatter_kernel, count), in_specs=[IN_HBM...  83.4 us
    pallas_call x1, Pallas kernels, gather_all(): pl.pallas_call(functools.partial(gather_kernel, count), in_specs=[IN_HBM]...  77.8 us
    pallas_call x1, Pallas kernels, ffn(): pl.pallas_call(ffn_kernel, in_specs=[IN_VMEM] * 8, out_specs=[IN_VMEM] *...  57 us
    pallas_call x3, Pallas kernels, whole(): pl.pallas_call(kernel, in_specs=[IN_VMEM] * len(arrays) + [pl.BlockSpec(m...  33 us
    pallas_call x1, Pallas kernels, attend_back(): pl.pallas_call(attend_back_kernel, grid=(2, H // 2), in_specs=[pair_block...  20.1 us
    pallas_call x1, Pallas kernels, attend(): pl.pallas_call(attend_kernel, grid=(2, H // 2), in_specs=[pair_block(0),...  19 us

profile of v1, /device:TPU:0, one launch (start us, length us, event | category | flops | bytes accessed | tf_op | source)
XLA Modules:
  0.0 310.7 jit_solution(6214323654225096855)
XLA Ops:
  0.7 1.4 fusion.3
  6.6 8.6 %entry.1 = (f32[1024,768]{1,0:T(8,128)}, bf16[1024,768]{1,0:T(8,128)(2,1)}, bf16[1024,768]{1,0:T(8,128)(2,1)}, f32[2,512,512]{2,1,0:T(8,128)}, f32[1024,128]{1,0:T(8,128)}) custom-call(bf16[1024,768]{1,0:T(8,128)(2,1)} %feat_ref.1, bf16[1024,768]{1,0:T(8,128)(2,1)} %pos_ref.1, bf16[1024,768]{1,0:T(8,128)(2,1)} %cot_ref.1, s32[1,1024]{1,0:T(1,128)} %seg_ref.1, ...), custom_call_target="tpu_custom_call" | custom-call | tf_op jit(solution)/shard_map/entry/pallas_call | solution.py:695
  15.3 0.1 reshape.79
  15.4 0.6 fusion.refs_0_
  16.0 77.8 %gather.1 = (f32[256,256]{1,0:T(8,128)}, bf16[768,2304]{1,0:T(8,128)(2,1)}, bf16[768,768]{1,0:T(8,128)(2,1)}, bf16[768,3072]{1,0:T(8,128)(2,1)}, bf16[3072,768]{1,0:T(8,128)(2,1)}) custom-call(f32[8,256]{1,0:T(8,128)} %fusion.refs_0_, f32[24,2304]{1,0:T(8,128)} %refs_0_.1, f32[24,768]{1,0:T(8,128)} %refs_4_.3, f32[24,3072]{1,0:T(8,128)} %refs_8_.1, ...), custom_call_target="tpu_custom_call" | custom-call | tf_op jit(solution)/shard_map/gather/pallas_call | solution.py:247
  93.7 1.0 slice.72
  94.7 0.1 reshape_squeeze.9
  94.8 0.6 broadcast_in_dim.27.bias_ref
  95.5 8.5 %qkv.1.q_ref.k_ref.v_ref = bf16[1024,2304]{1,0:T(8,128)(2,1)} custom-call(bf16[1024,768]{1,0:T(8,128)(2,1)} %get-tuple-element.74.low_ref, bf16[768,2304]{1,0:T(8,128)(2,1)} %get-tuple-element.75.weight_ref, f32[1,2304]{1,0:T(1,128)} %broadcast_in_dim.27.bias_ref), custom_call_target="tpu_custom_call" | custom-call | tf_op jit(solution)/shard_map/qkv/pallas_call | solution.py:695
  103.9 19.0 %attend.1 = (bf16[1024,768]{1,0:T(8,128)(2,1)}, bf16[24,512,512]{2,1,0:T(8,128)(2,1)}) custom-call(bf16[1024,2304]{1,0:T(8,128)(2,1)} %qkv.1.q_ref.k_ref.v_ref, bf16[1024,2304]{1,0:T(8,128)(2,1)} %qkv.1.q_ref.k_ref.v_ref, bf16[1024,2304]{1,0:T(8,128)(2,1)} %qkv.1.q_ref.k_ref.v_ref, f32[2,512,512]{2,1,0:T(8,128)} %get-tuple-element.77.bias_ref), custom_call_target="tpu_custom_call" | custom-call | tf_op jit(solution)/shard_map/attend/pallas_call | solution.py:540
  122.9 0.1 slice.60
  123.0 0.9 slice.77
  123.9 0.1 copy.63
  124.0 0.1 copy.58
  124.1 0.1 reshape.82
  124.2 0.6 concatenate.10.vec_ref
  124.8 0.6 slice.79
  125.4 57.0 %ffn.1 = (bf16[1024,768]{1,0:T(8,128)(2,1)}, f32[1024,768]{1,0:T(8,128)}, bf16[1024,768]{1,0:T(8,128)(2,1)}, bf16[768,768]{1,0:T(8,128)(2,1)}, bf16[768,3072]{1,...) custom-call(bf16[1024,768]{1,0:T(8,128)(2,1)} %get-tuple-element.78.ctx_ref, ...), custom_call_target="tpu_custom_call" | custom-call | tf_op jit(solution)/shard_map/ffn/pallas_call | solution.py:643
  182.4 20.1 %attend_back.1 = (bf16[1024,768]{1,0:T(8,128)(2,1)}, bf16[1024,768]{1,0:T(8,128)(2,1)}, bf16[1024,768]{1,0:T(8,128)(2,1)}) custom-call(bf16[1024,2304]{1,0:T(8,128)(2,1)} %qkv.1.q_ref.k_ref.v_ref, bf16[1024,2304]{1,0:T(8,128)(2,1)} %qkv.1.q_ref.k_ref.v_ref, bf16[1024,2304]{1,0:T(8,128)(2,1)} %qkv.1.q_ref.k_ref.v_ref, ...), custom_call_target="tpu_custom_call" | custom-call | tf_op jit(solution)/shard_map/attend_back/pallas_call | solution.py:552
  202.6 15.9 %tail.1 = (bf16[768,2304]{1,0:T(8,128)(2,1)}, bf16[1024,768]{1,0:T(8,128)(2,1)}, bf16[1024,768]{1,0:T(8,128)(2,1)}, f32[8,768]{1,0:T(8,128)}) custom-call(bf16[1024,768]{1,0:T(8,128)(2,1)} %get-tuple-element.74.low_ref, bf16[1024,768]{1,0:T(8,128)(2,1)} %get-tuple-element.86.dq_ref, bf16[1024,768]{1,0:T(8,128)(2,1)} %get-tuple-element.87.dk_ref, ...), custom_call_target="tpu_custom_call" | custom-call | tf_op jit(solution)/shard_map/tail/pallas_call | solution.py:695
  218.4 0.8 slice_reduce_fusion.4
  219.4 0.1 reshape.83
  219.5 0.1 reshape.84
  219.6 0.1 copy.59
  219.9 0.7 pad_bitcast_fusion.refs_4_
  220.6 83.4 %scatter.1 = (f32[96,768]{1,0:T(8,128)}, f32[24,3072]{1,0:T(8,128)}, f32[24,768]{1,0:T(8,128)}, f32[24,2304]{1,0:T(8,128)}, f32[8,256]{1,0:T(8,128)}) custom-call(bf16[3072,768]{1,0:T(8,128)(2,1)} %get-tuple-element.94.refs_0_, bf16[768,3072]{1,0:T(8,128)(2,1)} %get-tuple-element.95.refs_1_, bf16[768,768]{1,0:T(8,128)(2,1)} %get-tuple-element.96.refs_2_, ...), custom_call_target="tpu_custom_call" | custom-call | tf_op jit(solution)/shard_map/scatter/pallas_call | solution.py:444
  304.0 4.0 %update.1 = (f32[24,2304]{1,0:T(8,128)}, f32[24,2304]{1,0:T(8,128)}, f32[24,2304]{1,0:T(8,128)}, f32[24,2304]{1,0:T(8,128)}, f32[24,768]{1,0:T(8,128)}, /*index=...) custom-call(f32[24,2304]{1,0:T(8,128)} %refs_0_.1, ...), custom_call_target="tpu_custom_call" | custom-call | tf_op jit(solution)/shard_map/update/pallas_call | solution.py:684
  308.1 0.7 slice_reduce_fusion.6
  308.7 0.1 reshape_squeeze.11
  308.8 0.6 add_multiply_fusion.1
  309.4 0.7 slice.71
  310.1 0.6 add_multiply_fusion
  (46 shorter events, 0.3 us)
Async XLA Ops:
  6.6 8.7 %copy-start.2 = (f32[2,24]{1,0:T(2,128)S(1)}, f32[2,24]{1,0:T(2,128)}, u32[]{:S(2)}) copy-start(f32[2,24]{1,0:T(2,128)} %param.32) | copy-start | bytes 580
  6.6 8.7 %copy-start.3 = (f32[240]{0:T(256)S(1)}, f32[240]{0:T(256)}, u32[]{:S(2)}) copy-start(f32[240]{0:T(256)} %param.33) | copy-start | bytes 2884
  202.5 16.8 %copy-start = (f32[8,768]{1,0:T(8,128)S(1)}, f32[8,768]{1,0:T(8,128)}, u32[]{:S(2)}) copy-start(f32[8,768]{1,0:T(8,128)} %get-tuple-element.99) | copy-start | bytes 73732
  202.6 16.8 %copy-start.1 = (f32[1,3072]{1,0:T(1,128)S(1)}, f32[1,3072]{1,0:T(1,128)}, u32[]{:S(2)}) copy-start(f32[1,3072]{1,0:T(1,128)} %get-tuple-element.100) | copy-start | bytes 36868
  304.0 4.8 %copy-start.5 = (f32[2,24]{1,0:T(2,128)S(1)}, f32[2,24]{1,0:T(2,128)}, u32[]{:S(2)}) copy-start(f32[2,24]{1,0:T(2,128)} %param.44) | copy-start | bytes 580
  304.0 4.8 %copy-start.6 = (f32[2,24]{1,0:T(2,128)S(1)}, f32[2,24]{1,0:T(2,128)}, u32[]{:S(2)}) copy-start(f32[2,24]{1,0:T(2,128)} %param.38) | copy-start | bytes 580
  304.0 6.1 %copy-start.7 = (f32[240]{0:T(256)S(1)}, f32[240]{0:T(256)}, u32[]{:S(2)}) copy-start(f32[240]{0:T(256)} %param.45) | copy-start | bytes 2884
  304.0 6.1 %copy-start.8 = (f32[240]{0:T(256)S(1)}, f32[240]{0:T(256)}, u32[]{:S(2)}) copy-start(f32[240]{0:T(256)} %param.39) | copy-start | bytes 2884
  308.8 1.9 copy-start.9
  310.1 0.6 copy-start.4

commit v2 on v1

--- a/solution.py
+++ b/solution.py
@@ -14,6 +14,8 @@
 FF = 3072
 TOK = 1024
 HALF = 512
+ROWS = 256
+COLS = 768
 
 EPSILON = 1e-05
 MASKED = -1000000000.0
@@ -67,9 +69,9 @@
         y = 1 - self.y if dy else self.y
         return zz * 4 + y * 2 + x
 
-    def greet(self):
+    def greet(self, *more):
         barrier = pltpu.get_barrier_semaphore()
-        for other in (self.partner, self.xn, self.yn):
+        for other in (self.partner, self.xn, self.yn, *more):
             pl.semaphore_signal(barrier, inc=1, device_id=(other,), device_id_type=MESH)
 
         @pl.when(self.z < 3)
@@ -81,7 +83,7 @@
             pl.semaphore_signal(barrier, inc=1, device_id=(self.down,), device_id_type=MESH)
 
         ends = jnp.where((self.z == 0) | (self.z == 3), 4, 5)
-        pl.semaphore_wait(barrier, ends)
+        pl.semaphore_wait(barrier, ends + len(more))
 
 
 def remote(src, dst, send, recv, other):
@@ -227,32 +229,6 @@
 
 
 GATHER_SCRATCH = 13
-
-
-def gather_kernel(count, *refs):
-    shards, fulls, rest = refs[:count], refs[count : 2 * count], refs[2 * count :]
-    place = Place()
-    place.greet()
-    jobs = [Gather(place, shards[i], fulls[i], rest[i * GATHER_SCRATCH : (i + 1) * GATHER_SCRATCH]) for i in range(count)]
-    for job in jobs:
-        job.load()
-    for t in range(count + 6):
-        for i, job in enumerate(jobs):
-            if 0 <= t - i <= 6:
-                job.step(t - i)
-
-
-def gather_all(shards, dtypes):
-    count = len(shards)
-    return pl.pallas_call(
-        functools.partial(gather_kernel, count),
-        in_specs=[IN_HBM] * count,
-        out_specs=[IN_HBM] * count,
-        out_shape=[S((32 * s.shape[0], s.shape[1]), d) for s, d in zip(shards, dtypes)],
-        scratch_shapes=sum([Gather.scratch(*s.shape, d) for s, d in zip(shards, dtypes)], []),
-        compiler_params=params(collective_id=0, has_side_effects=True),
-        name="gather",
-    )(*shards)
 
 
 class Scatter:
@@ -415,104 +391,70 @@
 SCATTER_SCRATCH = 17
 
 
-def scatter_kernel(count, *refs):
-    inputs, outs, rest = refs[:count], refs[count : 2 * count], refs[2 * count :]
-    place = Place()
-    place.greet()
-    each = SCATTER_SCRATCH + 2
-    jobs, loads = [], []
-    for i in range(count):
-        held, load, *own = rest[i * each : (i + 1) * each]
-        jobs.append(Scatter(place, held, outs[i], own))
-        loads.append(pltpu.make_async_copy(inputs[i], held, load))
-        loads[-1].start()
-    for t in range(count + 7):
-        for i, job in enumerate(jobs):
-            s = t - i
-            if s == 0:
-                loads[i].wait()
-            if 0 <= s <= 7:
-                job.step(s)
-
-
-def scatter_all(grads):
-    count = len(grads)
-    scratch = []
-    for g in grads:
-        scratch += [pltpu.VMEM(g.shape, g.dtype), DMA(())]
-        scratch += Scatter.scratch(g.shape[0] // 32, g.shape[1], g.dtype)
-    return pl.pallas_call(
-        functools.partial(scatter_kernel, count),
-        in_specs=[IN_HBM] * count,
-        out_specs=[IN_VMEM] * count,
-        out_shape=[S((g.shape[0] // 32, g.shape[1]), f32) for g in grads],
-        scratch_shapes=scratch,
-        compiler_params=params(collective_id=1, has_side_effects=True),
-        name="scatter",
-    )(*grads)
-
-
-def rotation(segments):
-    counts = [jnp.sum((segments == u).astype(jnp.int32)) for u in range(3)]
-    before, start = jnp.int32(0), jnp.int32(0)
-    taken = jnp.bool_(False)
-    for u in range(4):
-        here = (counts[u] == HALF) & ~taken if u < 3 else ~taken
-        start = jnp.where(here, before, start)
-        taken = taken | here
-        if u < 3:
-            before = before + counts[u]
-    return start
+def events(plan, it):
+    for at, steps in plan.items():
+
+        def now(steps=steps):
+            for step in steps:
+                step()
+
+        pl.when(it == at)(now)
+
+
+def looped(count, body, plan=None):
+    @pl.loop(0, count)
+    def _(it):
+        if plan:
+            events(plan, it)
+        body(it)
+
+
+def paced(steps, count, first=0):
+    plan = {}
+    for n, step in enumerate(steps):
+        plan.setdefault(first + n * (count - first) // len(steps), []).append(step)
+    return plan
+
+
+def tile(t, size):
+    return pl.ds(pl.multiple_of(t * size, size), size)
+
+
+def rotation(seg):
+    counts = [jnp.sum(jnp.where(seg == u, 1.0, 0.0), 1, keepdims=True) for u in range(3)]
+    start = counts[0] + counts[1] + counts[2]
+    start = jnp.where(counts[2] == HALF, counts[0] + counts[1], start)
+    start = jnp.where(counts[1] == HALF, counts[0], start)
+    return jnp.where(counts[0] == HALF, 0.0, start)
+
+
+def turn(t, start, back):
+    row = (lax.broadcasted_iota(jnp.int32, (ROWS, TOK), 0) + t * ROWS).astype(f32)
+    col = lax.broadcasted_iota(jnp.int32, (ROWS, TOK), 1).astype(f32)
+    source = row - start if back else row + start
+    source = jnp.where(source < 0.0, source + TOK, jnp.where(source >= TOK, source - TOK, source))
+    return jnp.where(source == col, 1.0, 0.0).astype(bf16)
 
 
 def column_of(row):
     return jnp.broadcast_to(row, (128, row.shape[1])).T
 
 
-def entry_kernel(feat_ref, pos_ref, cot_ref, seg_ref, valid_ref, start_ref, entry_ref, low_ref, cot_out_ref, bias_ref, valid_out_ref):
-    back = lax.rem(TOK - start_ref[0], TOK)
-    valid = valid_ref[...].astype(f32)
-    seg = seg_ref[...].astype(f32)
-    entry = (feat_ref[...].astype(f32) + pos_ref[...].astype(f32)) * column_of(valid)[:, :1]
-    entry = pltpu.roll(entry, back, 0)
-    entry_ref[...] = entry
-    low_ref[...] = entry.astype(bf16)
-    cot_out_ref[...] = pltpu.roll(cot_ref[...], back, 0)
-    valid = pltpu.roll(jnp.broadcast_to(valid, (8, TOK)), back, 1)[:1]
-    seg = pltpu.roll(jnp.broadcast_to(seg, (8, TOK)), back, 1)[:1]
-    valid_out_ref[...] = column_of(valid)
-    for h in range(2):
-        part = slice(h * HALF, (h + 1) * HALF)
-        seg_col = column_of(seg[:, part])[:, :1]
-        same = seg_col == seg[:, part]
-        rows = lax.broadcasted_iota(jnp.int32, (HALF, HALF), 0)
-        cols = lax.broadcasted_iota(jnp.int32, (HALF, HALF), 1)
-        allowed = same & ((valid[:, part] > 0.0) | (rows == cols))
-        bias_ref[h] = jnp.where(allowed, 0.0, MASKED)
-
-
-def qkv_kernel(low_ref, weight_ref, bias_ref, out_ref):
-    for k in range(3):
-        part = slice(k * D, (k + 1) * D)
-        out_ref[:, part] = (dot(low_ref[...], weight_ref[:, part], NN) + bias_ref[:, part]).astype(bf16)
-
-
-def attend_kernel(q_ref, k_ref, v_ref, bias_ref, out_ref, prob_ref):
-    q, k, v = q_ref[...] * jnp.bfloat16(0.125), k_ref[...], v_ref[...]
+def attend_pair(q, k, v, bias, prob_ref):
+    q = q * jnp.bfloat16(0.125)
     outs = []
     for h in range(2):
         qh = jnp.where(lane_half(h, q.shape), q, jnp.bfloat16(0))
-        scores = dot(qh, k, NT) + bias_ref[0]
+        scores = dot(qh, k, NT) + bias
         scores = jnp.exp(scores - jnp.max(scores, 1, keepdims=True))
         probs = (scores * (1.0 / jnp.sum(scores, 1, keepdims=True))).astype(bf16)
         prob_ref[h] = probs
         outs.append(dot(probs, v, NN))
-    out_ref[...] = jnp.where(lane_half(0, outs[0].shape), outs[0], outs[1]).astype(bf16)
-
-
-def attend_back_kernel(q_ref, k_ref, v_ref, grad_ref, ctx_ref, prob_ref, dq_ref, dk_ref, dv_ref):
-    q, k, v, grad = q_ref[...], k_ref[...], v_ref[...], grad_ref[...]
-    product = grad.astype(f32) * ctx_ref[...].astype(f32)
+    return jnp.where(lane_half(0, outs[0].shape), outs[0], outs[1]).astype(bf16)
+
+
+def attend_pair_back(q, k, v, grad, ctx, prob_ref):
+    product = grad.astype(f32) * ctx.astype(f32)
     dq, dk, dv = [], [], []
     for h in range(2):
         lanes = lane_half(h, grad.shape)
@@ -524,44 +466,172 @@
         dk.append(dot(ds, q, TN))
         dv.append(dot(probs, grad, TN))
     lanes = lane_half(0, grad.shape)
-    dq_ref[...] = (jnp.where(lanes, dq[0], dq[1]) * 0.125).astype(bf16)
-    dk_ref[...] = (jnp.where(lanes, dk[0], dk[1]) * 0.125).astype(bf16)
-    dv_ref[...] = jnp.where(lanes, dv[0], dv[1]).astype(bf16)
-
-
-def pair_block(offset):
-    return pl.BlockSpec((HALF, 2 * HD), lambda i, j: (i, offset + j))
-
-
-PROBS = pl.BlockSpec((2, HALF, HALF), lambda i, j: (i * (H // 2) + j, 0, 0))
-
-
-def attend(qkv, bias):
+    return [
+        (jnp.where(lanes, dq[0], dq[1]) * 0.125).astype(bf16),
+        (jnp.where(lanes, dk[0], dk[1]) * 0.125).astype(bf16),
+        jnp.where(lanes, dv[0], dv[1]).astype(bf16),
+    ]
+
+
+def bias_row(small_ref, first, bias_len):
+    total = jnp.zeros((8, 1024), f32)
+    lanes = lax.broadcasted_iota(jnp.int32, (8, 256), 1)
+    for d in range(first // bias_len, (first + D - 1) // bias_len + 1):
+        piece = jnp.where(lanes < bias_len, jnp.broadcast_to(small_ref[8 * d : 8 * d + 1, :], (8, 256)), 0.0)
+        piece = jnp.concatenate([piece, jnp.zeros((8, 768), f32)], axis=1)
+        shift = (bias_len * d - first) % 1024
+        total = total + (pltpu.roll(piece, shift, 1) if shift else piece)
+    return total[:1, :D]
+
+
+PAIRS = H // 2
+
+
+def entry_tile(t, start, stack, feat, pos, cot, entry, low, cot_out):
+    rows = tile(t, ROWS)
+    matrix = turn(t, start, False)
+    valid = dot(matrix, stack, NT)[:, 0:1]
+    value = (dot(matrix, feat[...], NN) + dot(matrix, pos[...], NN)) * valid
+    entry[rows, :] = value
+    low[rows, :] = value.astype(bf16)
+    cot_out[rows, :] = dot(matrix, cot[...], NN).astype(bf16)
+
+
+def mask_half(h, start, stack, mask):
+    matrix = jnp.concatenate([turn(2 * h, start, False), turn(2 * h + 1, start, False)], axis=0)
+    by_row = dot(stack, matrix, NT)
+    by_col = dot(matrix, stack, NT)
+    rows = lax.broadcasted_iota(jnp.int32, (HALF, HALF), 0)
+    cols = lax.broadcasted_iota(jnp.int32, (HALF, HALF), 1)
+    allowed = (by_col[:, 1:2] == by_row[1:2, :]) & ((by_row[0:1, :] > 0.0) | (rows == cols))
+    mask[h] = jnp.where(allowed, 0.0, MASKED)
+
+
+def stack_of(valid, seg):
+    row = lax.broadcasted_iota(jnp.int32, (8, TOK), 0)
+    both = jnp.where(row == 0, valid.astype(f32), jnp.where(row == 1, seg.astype(f32), 0.0))
+    return both.astype(bf16)
+
+
+def front_kernel(linked, bias_len, *refs):
+    n = 5
+    shards, refs = refs[:n], refs[n:]
+    (feat_in, pos_in, cot_in, seg_ref, valid_ref), refs = refs[:5], refs[5:]
+    fulls, refs = refs[:n], refs[n:]
+    (entry_out, low_out, cot_out, qkv_out, ctx_out, prob_out), refs = refs[:6], refs[6:]
+    (feat, pos, cot_raw, entry, low, cot, mask, small, weight, bias, qkv, ctx, probs, ins, outs, psem), refs = refs[:16], refs[16:]
+    loads = [pltpu.make_async_copy(a, b, ins.at[i]) for i, (a, b) in enumerate(((feat_in, feat), (pos_in, pos), (cot_in, cot_raw)))]
+    stores = [
+        pltpu.make_async_copy(a, b, outs.at[i])
+        for i, (a, b) in enumerate(((entry, entry_out), (low, low_out), (cot, cot_out), (qkv, qkv_out), (ctx, ctx_out), (small, fulls[0]), (weight, fulls[1])))
+    ]
+    for copy in loads:
+        copy.start()
+    plans = [{}, {}, {}, {}]
+    if linked:
+        place = Place()
+        place.greet()
+        homes = [small, weight, *fulls[2:]]
+        jobs = [Gather(place, shards[i], homes[i], refs[i * GATHER_SCRATCH : (i + 1) * GATHER_SCRATCH]) for i in range(n)]
+        for job in jobs:
+            job.load()
+        step = lambda i, s: functools.partial(jobs[i].step, s)
+        step(1, 0)()
+        step(0, 0)()
+        waves = [[(1, 1), (0, 1)], [(1, 2), (0, 2)], [(1, 3), (0, 3), (2, 0), (3, 0)], [(1, 4), (0, 4)], [(1, 5), (0, 5)], [(1, 6), (0, 6)]]
+        before = [step(*e) for wave in waves for e in wave]
+        plans[0] = paced(before[:4], 4)
+        middle, late = before[4:10], before[10:]
+        after = [
+            (2, 1), (3, 1), (4, 0), (2, 2), (3, 2), (2, 3), (4, 1), (3, 3), (2, 4), (4, 2), (3, 4), (2, 5), (4, 3), (3, 5), (2, 6), (4, 4), (3, 6), (4, 5), (4, 6),
+        ]
+        after = [step(*e) for e in after]
+        plans[2] = paced(after[:7], 9)
+        plans[3] = paced(after[7:17], 2 * PAIRS)
+        end = after[17:]
+    else:
+        middle, late, end = [], [], []
+        for i, (a, b) in enumerate(((shards[0], small), (shards[1], weight))):
+            copy = pltpu.make_async_copy(a, b, psem.at[i])
+            copy.start()
+            copy.wait()
+    for copy in loads:
+        copy.wait()
+    seg = seg_ref[...]
+    start = rotation(seg)
+    stack = stack_of(valid_ref[...], seg)
+    looped(4, lambda t: entry_tile(t, start, stack, feat, pos, cot_raw, entry, low, cot), plans[0])
+    for copy in stores[:3]:
+        copy.start()
+    for h in range(2):
+        for run in middle[3 * h : 3 * h + 3]:
+            run()
+        mask_half(h, start, stack, mask)
+    for run in late:
+        run()
+    bias[0:1, 0:D] = bias_row(small, 0, bias_len)
+    bias[0:1, D : 2 * D] = jnp.zeros((1, D), f32)
+    bias[0:1, 2 * D : 3 * D] = bias_row(small, D, bias_len)
+    if linked:
+        for copy in stores[5:]:
+            copy.start()
+
+    def project(t):
+        cols = tile(t, 256)
+        qkv[:, cols] = (dot(low[...], weight[:, cols], NN) + bias[0:1, cols]).astype(bf16)
+
+    looped(9, project, plans[2])
+    stores[3].start()
+
+    def prob_store(it):
+        return pltpu.make_async_copy(probs.at[it % 2], prob_out.at[pl.ds(2 * it, 2)], psem.at[it % 2])
+
+    def attention(it):
+        half, pair = it // PAIRS, it % PAIRS
+        rows = tile(half, HALF)
+        cut = lambda which: qkv[rows, tile(which * PAIRS + pair, 2 * HD)]
+
+        @pl.when(it >= 2)
+        def _():
+            prob_store(it - 2).wait()
+
+        ctx[rows, tile(pair, 2 * HD)] = attend_pair(cut(0), cut(1), cut(2), mask[half], probs.at[it % 2])
+        prob_store(it).start()
+
+    looped(2 * PAIRS, attention, plans[3])
+    stores[4].start()
+    for run in end:
+        run()
+    prob_store(2 * PAIRS - 2).wait()
+    prob_store(2 * PAIRS - 1).wait()
+    for copy in stores[: 7 if linked else 5]:
+        copy.wait()
+
+
+def front(linked, bias_len, shards, features, pos_conv, cotangent, segments, valid):
+    dtypes = [f32] + [bf16] * 4
+    fulls = [S((32 * s.shape[0], s.shape[1]) if linked else (8, 128), d) for s, d in zip(shards, dtypes)]
+    small_shape = (256, 256) if linked else shards[0].shape
+    scratch = [
+        pltpu.VMEM((TOK, D), bf16), pltpu.VMEM((TOK, D), bf16), pltpu.VMEM((TOK, D), bf16),
+        pltpu.VMEM((TOK, D), f32), pltpu.VMEM((TOK, D), bf16), pltpu.VMEM((TOK, D), bf16),
+        pltpu.VMEM((2, HALF, HALF), f32), pltpu.VMEM(small_shape, f32), pltpu.VMEM((D, 3 * D), bf16), pltpu.VMEM((8, 3 * D), f32),
+        pltpu.VMEM((TOK, 3 * D), bf16), pltpu.VMEM((TOK, D), bf16), pltpu.VMEM((2, 2, HALF, HALF), bf16),
+        DMA((3,)), DMA((7,)), DMA((2,)),
+    ]
+    if linked:
+        scratch += sum([Gather.scratch(*s.shape, d) for s, d in zip(shards, dtypes)], [])
+    more = dict(collective_id=0, has_side_effects=True) if linked else {}
     return pl.pallas_call(
-        attend_kernel,
-        grid=(2, H // 2),
-        in_specs=[pair_block(0), pair_block(H // 2), pair_block(H), pl.BlockSpec((1, HALF, HALF), lambda i, j: (i, 0, 0))],
-        out_specs=[pair_block(0), PROBS],
-        out_shape=[S((TOK, D), bf16), S((2 * H, HALF, HALF), bf16)],
-        compiler_params=params(),
-        name="attend",
-    )(qkv, qkv, qkv, bias)
-
-
-def attend_back(qkv, grad, ctx, probs):
-    return pl.pallas_call(
-        attend_back_kernel,
-        grid=(2, H // 2),
-        in_specs=[pair_block(0), pair_block(H // 2), pair_block(H), pair_block(0), pair_block(0), PROBS],
-        out_specs=[pair_block(0)] * 3,
-        out_shape=[S((TOK, D), bf16)] * 3,
-        compiler_params=params(),
-        name="attend_back",
-    )(qkv, qkv, qkv, grad, ctx, probs)
-
-
-ROWS = 256
-COLS = 768
+        functools.partial(front_kernel, linked, bias_len),
+        in_specs=[IN_HBM] * 8 + [IN_VMEM] * 2,
+        out_specs=[IN_HBM] * 11,
+        out_shape=fulls
+        + [S((TOK, D), f32), S((TOK, D), bf16), S((TOK, D), bf16), S((TOK, 3 * D), bf16), S((TOK, D), bf16), S((2 * H, HALF, HALF), bf16)],
+        scratch_shapes=scratch,
+        compiler_params=params(**more),
+        name="front",
+    )(*shards, features, pos_conv, cotangent, segments, valid)
 
 
 def normed_of(residual):
@@ -576,9 +646,9 @@
 
 
 def ffn_kernel(
-    ctx_ref, entry_ref, cot_ref, proj_ref, expand_ref, reduce_ref, vec_ref, b1_ref,
+    ctx_ref, entry_ref, cot_ref, proj_ref, expand_ref, reduce_ref, vec_ref, b1_ref, seg_ref,
     out_ref, first_ref, gctx_ref, dproj_ref, dexpand_ref, dreduce_ref, dvec_ref, db1_ref,
-    low_ref, act_ref, gffn_ref, gpre_ref, gbranch_ref, pre_ref, cdf_ref,
+    layer_ref, low_ref, act_ref, gffn_ref, gpre_ref, gbranch_ref, pre_ref, cdf_ref,
 ):
     dvec_ref[...] = jnp.zeros_like(dvec_ref)
     db1_ref[...] = jnp.zeros_like(db1_ref)
@@ -602,7 +672,7 @@
             act_ref[rows, cols] = act
             total = total + dot(act, reduce_ref[cols, :], NN)
         unit_2, scale_2 = normed_of(total)
-        out_ref[rows, :] = (unit_2 * g_2 + c_2).astype(bf16)
+        layer_ref[rows, :] = (unit_2 * g_2 + c_2).astype(bf16)
         grad = cot_ref[rows, :].astype(f32)
         dvec_ref[3:4, :] += jnp.sum(grad * unit_2, 0, keepdims=True)
         dvec_ref[5:6, :] += jnp.sum(grad, 0, keepdims=True)
@@ -627,6 +697,12 @@
         dvec_ref[0:1, :] += jnp.sum(branch.astype(f32), 0, keepdims=True)
         gctx_ref[rows, :] = dot(branch, proj_ref[...], NT).astype(bf16)
 
+    start = rotation(seg_ref[...])
+
+    @pl.loop(0, TOK // ROWS)
+    def _(t):
+        out_ref[tile(t, ROWS), :] = dot(turn(t, start, True), layer_ref[...], NN).astype(bf16)
+
     @pl.loop(0, FF // 256)
     def _(t):
         part = pl.ds(pl.multiple_of(t * 256, 256), 256)
@@ -642,14 +718,14 @@
 def ffn(*arrays):
     return pl.pallas_call(
         ffn_kernel,
-        in_specs=[IN_VMEM] * 8,
+        in_specs=[IN_VMEM] * 9,
         out_specs=[IN_VMEM] * 8,
         out_shape=[
             S((TOK, D), bf16), S((TOK, D), f32), S((TOK, D), bf16), S((D, D), bf16),
             S((D, FF), bf16), S((FF, D), bf16), S((8, D), f32), S((1, FF), f32),
         ],
         scratch_shapes=[
-            pltpu.VMEM((TOK, D), bf16), pltpu.VMEM((TOK, FF), bf16), pltpu.VMEM((TOK, D), bf16), pltpu.VMEM((TOK, FF), bf16),
+            pltpu.VMEM((TOK, D), bf16), pltpu.VMEM((TOK, D), bf16), pltpu.VMEM((TOK, FF), bf16), pltpu.VMEM((TOK, D), bf16), pltpu.VMEM((TOK, FF), bf16),
             pltpu.VMEM((TOK, D), bf16), pltpu.VMEM((ROWS, FF), f32), pltpu.VMEM((ROWS, FF), f32),
         ],
         compiler_params=pltpu.CompilerParams(vmem_limit_bytes=62 << 20),
@@ -657,16 +733,166 @@
     )(*arrays)
 
 
-def tail_kernel(low_ref, dq_ref, dk_ref, dv_ref, weight_ref, first_ref, valid_ref, out_ref, start_ref, grad_ref, input_ref, layer_ref, sums_ref):
-    total = first_ref[...]
-    for k, part_ref in enumerate((dq_ref, dk_ref, dv_ref)):
-        part = slice(k * D, (k + 1) * D)
-        grad_ref[:, part] = dot(low_ref[...], part_ref[...], TN).astype(bf16)
-        total = total + dot(part_ref[...], weight_ref[:, part], NT)
-        sums_ref[k : k + 1, :] = jnp.sum(part_ref[...].astype(f32), 0, keepdims=True)
-    total = (total * valid_ref[:, :1]).astype(bf16)
-    input_ref[...] = pltpu.roll(total, start_ref[0], 0)
-    layer_ref[...] = pltpu.roll(out_ref[...], start_ref[0], 0)
+class Exchange:
+    def __init__(self, place, total, slots, send, recv):
+        z = place.z
+        self.others = (place.partner, place.xn, place.yn, place.me + 8 - 16 * (z % 2), place.me + 16 - 32 * (z // 2))
+        self.total, self.slots, self.send, self.recv = total, slots, send, recv
+
+    def copy(self, n):
+        return remote(self.slots.at[n], self.slots.at[5 + n], self.send.at[n], self.recv.at[n], self.others[n])
+
+    def begin(self, n):
+        self.slots[n] = self.total[...]
+        self.copy(n).start()
+
+    def end(self, n):
+        self.copy(n).wait()
+        self.total[...] += self.slots[5 + n]
+
+
+VECTOR_ROWS = 72
+
+
+def put(vector, row, value):
+    for i in range(value.shape[1] // 128):
+        vector[row + i : row + i + 1, :] = value[:, 128 * i : 128 * (i + 1)]
+
+
+def back_kernel(linked, *refs):
+    n = 3
+    parts, refs = refs[:n], refs[n:]
+    (qkv_in, grad_in, ctx_in, prob_in, low_in, weight_in, first_in, dvec_ref, db1_ref, seg_ref, valid_ref), refs = refs[:11], refs[11:]
+    if linked:
+        outs, refs = refs[: n + 1], refs[n + 1 :]
+    else:
+        (qkv_part,), refs = refs[:1], refs[1:]
+    (vector, input_out), refs = refs[:2], refs[2:]
+    (qkv, grad, ctx, probs, low, weight, first, dqkv, inner, ins, psem), refs = refs[:11], refs[11:]
+    loads = [
+        pltpu.make_async_copy(a, b, ins.at[i])
+        for i, (a, b) in enumerate(((qkv_in, qkv), (grad_in, grad), (ctx_in, ctx), (low_in, low), (weight_in, weight), (first_in, first)))
+    ]
+
+    def prob_load(it):
+        return pltpu.make_async_copy(prob_in.at[pl.ds(2 * it, 2)], probs.at[it % 2], psem.at[it % 2])
+
+    for copy in loads[:3]:
+        copy.start()
+    prob_load(0).start()
+    plans = [{}, {}, {}]
+    end = []
+    if linked:
+        (slots, send, recv), refs = refs[:3], refs[3:]
+        each = SCATTER_SCRATCH + 1
+        place = Place()
+        held = [refs[i * each] for i in range(n + 1)]
+        jobs = [Scatter(place, held[i], outs[i], refs[i * each + 1 : (i + 1) * each]) for i in range(n + 1)]
+        swap = Exchange(place, vector, slots, send, recv)
+        fetch = [pltpu.make_async_copy(parts[i], held[i], ins.at[6 + i]) for i in range(n)]
+        for copy in fetch:
+            copy.start()
+        place.greet(swap.others[4])
+        for i in range(n):
+            fetch[i].wait()
+            jobs[i].step(0)
+        qkv_part = held[n]
+        r, e, p, q = jobs
+        do = lambda f, *a: functools.partial(f, *a)
+        plans[0] = paced(
+            [
+                do(r.pair, 3), do(r.pair, 2), do(r.pair, 1), do(r.side_on, 3), do(r.pair, 0), do(r.side_on, 2), do(e.pair, 3), do(r.side_on, 1),
+                do(e.pair, 2), do(r.side_on, 0), do(e.pair, 1), do(r.column, 3),
+            ],
+            2 * PAIRS,
+        )
+        plans[1] = paced([do(e.side_on, 3), do(e.pair, 0), do(r.column, 2), do(e.side_on, 2)], 9)
+        plans[2] = paced([do(e.side_on, 1), do(p.pair, 3), do(r.column, 1), do(e.side_on, 0)], 4)
+        end = [
+            do(p.pair, 2), do(p.pair, 1), do(e.column, 3), do(p.side_on, 3), do(p.pair, 0), do(r.total), do(p.side_on, 2), do(q.pair, 3), do(p.side_on, 1),
+            do(e.column, 2), do(q.pair, 2), do(p.side_on, 0), do(e.column, 1), do(q.side_on, 3), do(q.pair, 1), do(p.column, 3), do(q.side_on, 2), do(q.pair, 0),
+            do(e.total), do(p.column, 2), do(swap.end, 0), do(swap.begin, 1), do(q.side_on, 1), do(q.column, 3), do(p.column, 1),
+            do(swap.end, 1), do(swap.begin, 2), do(q.side_on, 0), do(q.column, 2), do(swap.end, 2), do(swap.begin, 3), do(p.total),
+            do(q.column, 1), do(swap.end, 3), do(swap.begin, 4), do(q.total), do(swap.end, 4), do(r.finish), do(e.finish), do(p.finish), do(q.finish),
+        ]
+    for copy in loads[3:]:
+        copy.start()
+    for copy in loads[:3]:
+        copy.wait()
+
+    def attention(it):
+        half, pair = it // PAIRS, it % PAIRS
+        rows = tile(half, HALF)
+        cut = lambda ref, which: ref[rows, tile(which * PAIRS + pair, 2 * HD)]
+
+        @pl.when(it < 2 * PAIRS - 1)
+        def _():
+            prob_load(it + 1).start()
+
+        prob_load(it).wait()
+        three = attend_pair_back(cut(qkv, 0), cut(qkv, 1), cut(qkv, 2), cut(grad, 0), cut(ctx, 0), probs.at[it % 2])
+        for which, value in enumerate(three):
+            dqkv[rows, tile(which * PAIRS + pair, 2 * HD)] = value
+
+    looped(2 * PAIRS, attention, plans[0])
+    for copy in loads[3:]:
+        copy.wait()
+
+    def weight_grad(t):
+        cols = tile(t, 256)
+        qkv_part[:, cols] = dot(low[...], dqkv[:, cols], TN).astype(bf16)
+
+    looped(9, weight_grad, plans[1])
+    for which, row in ((0, 0), (2, 6)):
+        put(vector, row, jnp.sum(dqkv[:, which * D : (which + 1) * D].astype(f32), 0, keepdims=True))
+    put(vector, 18, db1_ref[...])
+    for row, at in ((0, 12), (1, 42), (4, 48), (5, 54), (2, 60), (3, 66)):
+        put(vector, at, dvec_ref[row : row + 1, :])
+    if linked:
+        jobs[n].step(0)
+        swap.begin(0)
+
+    def input_grad(t):
+        rows = tile(t, ROWS)
+        inner[rows, :] = (first[rows, :] + dot(dqkv[rows, :], weight[...], NT)).astype(bf16)
+
+    looped(4, input_grad, plans[2])
+    start = rotation(seg_ref[...])
+
+    def turn_back(t):
+        rows = tile(t, ROWS)
+        input_out[rows, :] = dot(turn(t, start, True), inner[...], NN).astype(bf16)
+
+    looped(4, turn_back)
+    input_out[...] = input_out[...] * column_of(valid_ref[...].astype(f32))[:, :1].astype(bf16)
+    for run in end:
+        run()
+
+
+def back(linked, parts, *arrays):
+    shapes = [p.shape for p in parts] + [(D, 3 * D)]
+    outs = [S((r // 32, c), f32) for r, c in shapes] if linked else [S((D, 3 * D), bf16)]
+    outs += [S((VECTOR_ROWS, 128), f32), S((TOK, D), bf16)]
+    scratch = [
+        pltpu.VMEM((TOK, 3 * D), bf16), pltpu.VMEM((TOK, D), bf16), pltpu.VMEM((TOK, D), bf16), pltpu.VMEM((2, 2, HALF, HALF), bf16),
+        pltpu.VMEM((TOK, D), bf16), pltpu.VMEM((D, 3 * D), bf16), pltpu.VMEM((TOK, D), f32), pltpu.VMEM((TOK, 3 * D), bf16),
+        pltpu.VMEM((TOK, D), bf16), DMA((9,)), DMA((2,)),
+    ]
+    more = {}
+    if linked:
+        more = dict(collective_id=1, has_side_effects=True)
+        scratch += [pltpu.VMEM((10, VECTOR_ROWS, 128), f32), DMA((5,)), DMA((5,))]
+        for r, c in shapes:
+            scratch += [pltpu.VMEM((r, c), bf16)] + Scatter.scratch(r // 32, c, bf16)
+    return pl.pallas_call(
+        functools.partial(back_kernel, linked),
+        in_specs=[IN_HBM] * 10 + [IN_VMEM] * 4,
+        out_specs=[IN_VMEM] * len(outs),
+        out_shape=outs,
+        scratch_shapes=scratch,
+        compiler_params=params(**more),
+        name="back",
+    )(*parts, *arrays)
 
 
 def update_kernel(rates, *refs):
@@ -691,25 +917,8 @@
     )(*arrays)
 
 
-def whole(kernel, name, shapes, *arrays, scalars=()):
-    return pl.pallas_call(
-        kernel,
-        in_specs=[IN_VMEM] * len(arrays) + [pl.BlockSpec(memory_space=pltpu.SMEM)] * len(scalars),
-        out_specs=[IN_VMEM] * len(shapes),
-        out_shape=[S(*s) for s in shapes],
-        compiler_params=params(),
-        name=name,
-    )(*arrays, *scalars)
-
-
 def rounded(x):
     return lax.reduce_precision(x, 8, 7)
-
-
-def packed(bias_rows, gain_rows):
-    n = bias_rows.shape[0]
-    rows = jnp.stack([jnp.pad(r, ((0, 0), (0, 256 - r.shape[1]))) for r in (bias_rows, gain_rows)], axis=1)
-    return jnp.pad(rows, ((0, 0), (0, 6), (0, 0))).reshape(8 * n, 256)
 
 
 def local(linked, *args):
@@ -720,53 +929,41 @@
         qkv_average, proj_average, expand_average, reduce_average, gains_average, bias_average,
     ) = args
     ranks = lax.axis_size("dp")
+    me = lax.axis_index("dp")
     bias_len = bias_vector.shape[0]
     gain_len = norm_gains.shape[1]
-    shards = [qkv_weight, proj_weight, expand_weight, reduce_weight]
-    small = packed(rounded(bias_vector)[None], rounded(norm_gains).reshape(1, -1))
-    if linked:
-        small_full, qkv_full, proj_full, expand_full, reduce_full = gather_all([small] + shards, [f32] + [bf16] * 4)
-    else:
-        small_full, qkv_full, proj_full, expand_full, reduce_full = [
-            lax.all_gather(s, "dp", axis=0, tiled=True) for s in [small] + [w.astype(bf16) for w in shards]
-        ]
+    small = jnp.stack([jnp.pad(rounded(r), (0, 256 - r.shape[0])) for r in (bias_vector, norm_gains.reshape(-1))])
+    small = jnp.pad(small, ((0, 6), (0, 0)))
+    shards = [small, qkv_weight, proj_weight, expand_weight, reduce_weight]
+    if not linked:
+        shards = [lax.all_gather(s, "dp", axis=0, tiled=True) for s in [small] + [w.astype(bf16) for w in shards[1:]]]
+    *fulls, entry, entry_low, cot, qkv, ctx, probs = front(
+        linked, bias_len, shards, features, pos_conv, cotangent, segment_ids, frame_valid
+    )
+    small_full, qkv_full, proj_full, expand_full, reduce_full = fulls if linked else shards
     small_full = small_full.reshape(ranks, 8, 256)
     bias_full = small_full[:, 0, :bias_len].reshape(-1)
     gains_full = small_full[:, 1, : 2 * gain_len].reshape(ranks, 2, gain_len).transpose(1, 0, 2).reshape(2, D)
-    start = rotation(segment_ids)[None]
-    entry, entry_low, cot, mask, valid = whole(
-        entry_kernel,
-        "entry",
-        [((TOK, D), f32), ((TOK, D), bf16), ((TOK, D), bf16), ((2, HALF, HALF), f32), ((TOK, 128), f32)],
-        features, pos_conv, cotangent, segment_ids, frame_valid, scalars=(start,),
-    )
-    qkv_bias = jnp.concatenate([bias_full[:D], jnp.zeros((D,), f32), bias_full[D : 2 * D]])[None]
-    (qkv,) = whole(qkv_kernel, "qkv", [((TOK, 3 * D), bf16)], entry_low, qkv_full, qkv_bias)
-    ctx, probs = attend(qkv, mask)
     vectors = jnp.concatenate(
         [
             bias_full[2 * D : 3 * D][None], bias_full[3 * D + FF : 4 * D + FF][None], gains_full,
             bias_full[4 * D + FF :].reshape(2, D), jnp.zeros((2, D), f32),
         ]
     )
-    layer, first, grad_ctx, proj_part, expand_part, reduce_part, dvec, db1 = ffn(
-        ctx, entry, cot, proj_full, expand_full, reduce_full, vectors, bias_full[3 * D : 3 * D + FF][None]
+    layer_out, first, grad_ctx, proj_part, expand_part, reduce_part, dvec, db1 = ffn(
+        ctx, entry, cot, proj_full, expand_full, reduce_full, vectors, bias_full[3 * D : 3 * D + FF][None], segment_ids
     )
-    dq, dk, dv = attend_back(qkv, grad_ctx, ctx, probs)
-    qkv_part, grad_input, layer_out, sums = whole(
-        tail_kernel,
-        "tail",
-        [((D, 3 * D), bf16), ((TOK, D), bf16), ((TOK, D), bf16), ((8, D), f32)],
-        entry_low, dq, dk, dv, qkv_full, first, valid, layer, scalars=(start,),
+    parts = [reduce_part, expand_part, proj_part]
+    *sums, vector, grad_input = back(
+        linked, parts, qkv, grad_ctx, ctx, probs, entry_low, qkv_full, first, dvec, db1, segment_ids, frame_valid
     )
-    bias_part = jnp.concatenate([sums[0], sums[2], dvec[0], db1[0], dvec[1], dvec[4], dvec[5]]).reshape(ranks, bias_len)
-    gain_part = dvec[2:4].reshape(2, ranks, gain_len).transpose(1, 0, 2).reshape(ranks, 2 * gain_len)
-    parts = [reduce_part, expand_part, proj_part, qkv_part, packed(bias_part, gain_part)]
-    if linked:
-        parts = scatter_all(parts)
-    else:
-        parts = [lax.psum_scatter(p.astype(f32), "dp", scatter_dimension=0, tiled=True) for p in parts]
-    reduce_grad, expand_grad, proj_grad, qkv_grad, small_grad = parts
+    if not linked:
+        sums = [lax.psum_scatter(p.astype(f32), "dp", scatter_dimension=0, tiled=True) for p in parts + sums]
+        vector = lax.psum(vector, "dp")
+    reduce_grad, expand_grad, proj_grad, qkv_grad = sums
+    vector = vector.reshape(-1)
+    bias_grad = lax.dynamic_slice(vector, (me * bias_len,), (bias_len,))
+    gains_grad = lax.dynamic_slice(vector[6 * D + FF :].reshape(2, D), (0, me * gain_len), (2, gain_len))
     root = math.sqrt(ranks * features.shape[0])
     matrix, proj, little = rate_matrix / root, rate_proj / root, rate_small / root
     updated = update(
@@ -784,8 +981,8 @@
         renewed = master - little * (gradient + 0.5 * velocity)
         return gradient, renewed, velocity, 0.5 * average + 0.5 * renewed
 
-    gains_new = nesterov(norm_gains, small_grad[1, : 2 * gain_len].reshape(2, gain_len), gains_moment, gains_average)
-    bias_new = nesterov(bias_vector, small_grad[0, :bias_len], bias_moment, bias_average)
+    gains_new = nesterov(norm_gains, gains_grad, gains_moment, gains_average)
+    bias_new = nesterov(bias_vector, bias_grad, bias_moment, bias_average)
     results = [layer_out, grad_input]
     for i in range(4):
         results += [updated[i], updated[4 + i], updated[8 + i], updated[12 + i], gains_new[i], bias_new[i]]

time: 311 us -> 245 us (0.79)
  Pallas kernels: 294 us -> 234 us
  between operations: 5.53 us -> 0.83 us
    pallas_call x8 -> x3, Pallas kernels: 290 us -> 230 us  [the longest x1 89.7 us: front(): pl.pallas_call(functools.partial(front_kernel, linked, bias_len), in_spec...]
where the time goes in v2:
time: 245 us; the launch traced here: 244 us
  Pallas kernels  234 us (96%)
  local copies, waits for them, and re-layouts  5.58 us (2%)
  other arithmetic  3.98 us (2%)
    pallas_call x1, Pallas kernels, front(): pl.pallas_call(functools.partial(front_kernel, linked, bias_len), in_spec...  89.7 us
    pallas_call x1, Pallas kernels, back(): pl.pallas_call(functools.partial(back_kernel, linked), in_specs=[IN_HBM]...  80.7 us
    pallas_call x1, Pallas kernels, ffn(): pl.pallas_call(ffn_kernel, in_specs=[IN_VMEM] * 9, out_specs=[IN_VMEM] *...  59.6 us

profile of v2, /device:TPU:0, one launch (start us, length us, event | category | flops | bytes accessed | tf_op | source)
XLA Modules:
  0.0 244.5 jit_solution(8137124696233019241)
XLA Ops:
  0.7 0.7 reduce_precision.10
  1.4 0.1 reduce_precision.11
  1.4 0.7 reduce_precision.9
  2.1 0.6 select_maximum_fusion.refs_0_
  2.7 89.7 %front.1 = (f32[256,256]{1,0:T(8,128)}, bf16[768,2304]{1,0:T(8,128)(2,1)}, bf16[768,768]{1,0:T(8,128)(2,1)}, bf16[768,3072]{1,0:T(8,128)(2,1)}, bf16[3072,768]{1...) custom-call(f32[8,256]{1,0:T(8,128)} %select_maximum_fusion.refs_0_,, ...), custom_call_target="tpu_custom_call" | custom-call | tf_op jit(solution)/shard_map/front/pallas_call | solution.py:625
  92.5 1.0 slice.33
  93.5 0.1 reshape_squeeze.6
  93.6 0.1 slice.29
  93.7 0.9 slice.36
  94.6 0.1 copy.54
  94.7 0.1 copy.52
  94.8 0.1 reshape.72
  94.9 0.6 concatenate.3.vec_ref
  95.5 0.6 slice.38
  96.1 59.6 %ffn.1 = (bf16[1024,768]{1,0:T(8,128)(2,1)}, f32[1024,768]{1,0:T(8,128)}, bf16[1024,768]{1,0:T(8,128)(2,1)}, bf16[768,768]{1,0:T(8,128)(2,1)}, bf16[768,3072]{1,...) custom-call(bf16[1024,768]{1,0:T(8,128)(2,1)} %get-tuple-element.67.ctx_ref.refs_5_, ...), custom_call_target="tpu_custom_call" | custom-call | tf_op jit(solution)/shard_map/ffn/pallas_call | solution.py:719
  155.7 80.7 %back.1 = (f32[96,768]{1,0:T(8,128)}, f32[24,3072]{1,0:T(8,128)}, f32[24,768]{1,0:T(8,128)}, f32[24,2304]{1,0:T(8,128)}, f32[72,128]{1,0:T(8,128)}, /*index=5*/bf16[1024,768]{1,0:T(8,128)(2,1)}) custom-call(bf16[3072,768]{1,0:T(8,128)(2,1)} %get-tuple-element.75.refs_0_, bf16[768,3072]{1,0:T(8,128)(2,1)} %get-tuple-element.76.refs_1_, ...), custom_call_target="tpu_custom_call" | custom-call | tf_op jit(solution)/shard_map/back/pallas_call | solution.py:887
  236.4 0.0 copy-start.1
  236.4 0.0 copy-start.3
  236.4 0.0 copy-start.4
  236.4 0.0 copy-start.2
  236.4 0.0 copy-start.5
  236.5 0.0 copy-start.6
  236.5 0.0 copy-start
  236.5 4.1 %update.1 = (f32[24,2304]{1,0:T(8,128)}, f32[24,2304]{1,0:T(8,128)}, f32[24,2304]{1,0:T(8,128)}, f32[24,2304]{1,0:T(8,128)}, f32[24,768]{1,0:T(8,128)}, /*index=...) custom-call(f32[24,2304]{1,0:T(8,128)} %refs_0_.1, ...), custom_call_target="tpu_custom_call" | custom-call | tf_op jit(solution)/shard_map/update/pallas_call | solution.py:910
  240.6 0.7 slice.32
  241.3 0.0 copy-done.1
  241.3 0.0 copy-done.3
  241.3 0.0 copy-done.4
  241.3 0.7 add_multiply_fusion.1
  242.0 0.0 copy-done.6
  242.0 1.4 add_multiply_fusion
  243.3 1.1 copy.56
  (12 shorter events, 0.1 us)
Async XLA Ops:
  236.4 4.9 %copy-start.1 = (f32[2,24]{1,0:T(2,128)S(1)}, f32[2,24]{1,0:T(2,128)}, u32[]{:S(2)}) copy-start(f32[2,24]{1,0:T(2,128)} %param.32) | copy-start | bytes 580
  236.4 4.9 %copy-start.3 = (f32[2,24]{1,0:T(2,128)S(1)}, f32[2,24]{1,0:T(2,128)}, u32[]{:S(2)}) copy-start(f32[2,24]{1,0:T(2,128)} %param.44) | copy-start | bytes 580
  236.4 4.9 %copy-start.4 = (f32[2,24]{1,0:T(2,128)S(1)}, f32[2,24]{1,0:T(2,128)}, u32[]{:S(2)}) copy-start(f32[2,24]{1,0:T(2,128)} %param.38) | copy-start | bytes 580
  236.4 5.5 %copy-start.2 = (f32[240]{0:T(256)S(1)}, f32[240]{0:T(256)}, u32[]{:S(2)}) copy-start(f32[240]{0:T(256)} %param.33) | copy-start | bytes 2884
  236.4 5.5 %copy-start.5 = (f32[240]{0:T(256)S(1)}, f32[240]{0:T(256)}, u32[]{:S(2)}) copy-start(f32[240]{0:T(256)} %param.45) | copy-start | bytes 2884
  236.5 5.5 %copy-start.6 = (f32[240]{0:T(256)S(1)}, f32[240]{0:T(256)}, u32[]{:S(2)}) copy-start(f32[240]{0:T(256)} %param.39) | copy-start | bytes 2884
  236.5 6.9 %copy-start = (bf16[1024,768]{1,0:T(8,128)(2,1)S(1)}, bf16[1024,768]{1,0:T(8,128)(2,1)}, u32[]{:S(2)}) copy-start(bf16[1024,768]{1,0:T(8,128)(2,1)} %get-tuple-element.145) | copy-start | bytes 4718596
